TPU v7x, 256 devices: a whole 4x4x8 slice. The times are simulated.
256 devices in a mesh: page: 32 (over z, x), feat: 8 (over y, core).
Axes of the slice: x: 4, y: 4, z: 8, core: 2. Of those that a mesh axis runs over, the one named last changes fastest.
Arguments:
- queries: bfloat16 [256, 4096], P('page', 'feat')
- fresh_token_keys: bfloat16 [256, 2048], P('page', 'feat')
- fresh_token_values: bfloat16 [256, 2048], P('page', 'feat'), may hold values from -6 to 6
- paged_keys: bfloat16 [512, 256, 2048], P('page', None, 'feat'), may hold values from -6 to 6
- paged_values: bfloat16 [512, 256, 2048], P('page', None, 'feat'), may hold values from -6 to 6
- block_tables: int32 [256, 8], replicated, may hold values from -1 to 511, as said below
- parents: int32 [256], replicated, may hold values from 0 to 255, as said below
- prompt_lengths: int32 [32], replicated, may hold values from 1 to 2047, as said below
- stream: bfloat16 [256, 4608], P(('page', 'feat'))
- output_matrix: bfloat16 [4608, 4096], P(None, 'feat')
- attention_gain: bfloat16 [4608], replicated, may hold values from 0.5 to 1.5
- feedforward_gain: bfloat16 [4608], replicated, may hold values from 0.5 to 1.5
- gate_matrix: bfloat16 [36864, 4608], P(('page', 'feat')), may hold values from -0.09375 to 0.09375
- linear_matrix: bfloat16 [36864, 4608], P(('page', 'feat')), may hold values from -0.09375 to 0.09375
- down_matrix: bfloat16 [36864, 4608], P(('page', 'feat'))
- closing_gain: bfloat16 [4608], replicated, may hold values from 0.5 to 1.5
Outputs:
- layer_output: bfloat16 [256, 4608], P(('page', 'feat'))
Inputs may be any that keep to these rules, and one draw needn't show every extreme that they name: `block_tables`: row r's table lists the page slots of its blocks in order; entries from ceil(prompt_lengths[r // 8] / 256) on are -1. Rows of one prompt list the same slots for all but their last listed block, which is each row's own. A slot is listed by the rows of one prompt only, and at most once in a row. `prompt_lengths`: the new token of each prompt's rows stands at this position. `parents`: the parent of row r is a row of the same prompt, from 8 * (r // 8) to that plus 8 - 1.
All inputs are finite; a program needn't handle non-finite values.
Results may differ from a plain program's by a relative error of at most 0.0095.
Values may be sent and summed in bfloat16 or wider, within the bound.
No kernel may reach another device: no remote copies, remote signals or barrier semaphores. Data moves between devices by JAX's collectives and lax.ppermute only.
A program may use at most 64 MiB of HBM per device.

v0:
```python
import math

import jax
import jax.numpy as jnp
from jax import lax
from jax.sharding import PartitionSpec as P

HEAD_DIM_SIZE = 128
QSCALAR = 144
SOFTCAP = 50
BEAMS = 8


norm_eps = 1e-06


def capped(scores):
    return SOFTCAP * jnp.tanh(scores / SOFTCAP)


def normalize(values, gain_row):
    mean_square = jnp.mean(values * values, axis=1, keepdims=True)
    return values * lax.rsqrt(mean_square + norm_eps) * gain_row.astype(jnp.float32)[None, :]


def activate(segment, gate_matrix, linear_matrix):
    gate_sums = lax.dot_general(
        segment, gate_matrix, (((1,), (1,)), ((), ())), preferred_element_type=jnp.float32
    )
    lift_sums = lax.dot_general(
        segment, linear_matrix, (((1,), (1,)), ((), ())), preferred_element_type=jnp.float32
    )
    return (jax.nn.gelu(gate_sums, approximate=True) * lift_sums).astype(jnp.bfloat16)


def per_device(
    queries,
    fresh_token_keys,
    fresh_token_values,
    paged_keys,
    paged_values,
    block_tables,
    parents,
    prompt_lengths,
    stream,
    output_matrix,
    attention_gain,
    feedforward_gain,
    gate_matrix,
    linear_matrix,
    down_matrix,
    closing_gain,
):
    home_rows = queries.shape[0]
    slot_count = paged_keys.shape[0]
    page_len = paged_keys.shape[1]
    kv_heads = paged_keys.shape[2] // HEAD_DIM_SIZE
    query_groups = queries.shape[1] // HEAD_DIM_SIZE // kv_heads
    root_scale = math.sqrt(QSCALAR)
    all_queries = lax.all_gather(queries, "page", axis=0, tiled=True)
    row_count = all_queries.shape[0]
    row_tables = jnp.take(block_tables, parents, axis=0)
    slot_ids = lax.axis_index("page") * slot_count + jnp.arange(slot_count, dtype=jnp.int32)
    matches = row_tables[None, :, :] == slot_ids[:, None, None]
    in_use = jnp.any(matches, axis=2)
    block_index = jnp.arange(row_tables.shape[1], dtype=jnp.int32)
    block_pos = jnp.sum(jnp.where(matches, block_index[None, None, :], 0), axis=2)
    row_ids = jnp.arange(row_count, dtype=jnp.int32)
    owner_prompt = jnp.max(jnp.where(in_use, (row_ids // BEAMS)[None, :], -1), axis=1)
    prompt_ids = jnp.maximum(owner_prompt, 0)
    beam_rows = prompt_ids[:, None] * BEAMS + jnp.arange(BEAMS, dtype=jnp.int32)[None, :]
    row_in_use = jnp.take_along_axis(in_use, beam_rows, axis=1)
    row_block = jnp.take_along_axis(block_pos, beam_rows, axis=1)
    limits = jnp.take(prompt_lengths, prompt_ids)
    positions = (
        row_block[:, :, None] * page_len + jnp.arange(page_len, dtype=jnp.int32)[None, None, :]
    )
    visible = jnp.logical_and(row_in_use[:, :, None], positions < limits[:, None, None])
    slot_queries = jnp.take(all_queries, beam_rows.reshape(-1), axis=0).reshape(
        slot_count, BEAMS, kv_heads, query_groups, HEAD_DIM_SIZE
    )
    page_keys = paged_keys.reshape(slot_count, page_len, kv_heads, HEAD_DIM_SIZE)
    page_values = paged_values.reshape(slot_count, page_len, kv_heads, HEAD_DIM_SIZE)
    raw_scores = jnp.einsum(
        "sbkgd,stkd->sbkgt", slot_queries, page_keys, preferred_element_type=jnp.float32
    )
    weights = jnp.where(
        visible[:, :, None, None, :], jnp.exp(capped(raw_scores / root_scale)), jnp.float32(0.0)
    )
    slot_totals = jnp.sum(weights, axis=4)
    slot_numerators = jnp.einsum(
        "sbkgt,stkd->sbkgd",
        weights.astype(jnp.bfloat16),
        page_values,
        preferred_element_type=jnp.float32,
    )
    selector = (beam_rows[:, :, None] == row_ids[None, None, :]).astype(jnp.float32)
    numerator_rows = jnp.einsum(
        "avz,avo->zo",
        selector,
        slot_numerators.reshape(slot_count, BEAMS, -1),
        precision=lax.Precision.HIGHEST,
    )
    total_rows = jnp.einsum(
        "avz,avo->zo",
        selector,
        slot_totals.reshape(slot_count, BEAMS, -1),
        precision=lax.Precision.HIGHEST,
    )
    home_numerators, home_totals = (
        lax.psum_scatter(numerator_rows, "page", scatter_dimension=0, tiled=True),
        lax.psum_scatter(total_rows, "page", scatter_dimension=0, tiled=True),
    )
    own_queries = queries.reshape(home_rows, kv_heads, query_groups, HEAD_DIM_SIZE)
    own_keys = fresh_token_keys.reshape(home_rows, kv_heads, HEAD_DIM_SIZE)
    own_values = fresh_token_values.reshape(home_rows, kv_heads, HEAD_DIM_SIZE)
    self_weight = jnp.exp(
        capped(
            jnp.einsum("rkgd,rkd->rkg", own_queries, own_keys, preferred_element_type=jnp.float32)
            / root_scale
        )
    )
    totals = home_totals.reshape(home_rows, kv_heads, query_groups) + self_weight
    self_term = jnp.einsum(
        "rkg,rkd->rkgd",
        self_weight.astype(jnp.bfloat16),
        own_values,
        preferred_element_type=jnp.float32,
    )
    numerators = (
        home_numerators.reshape(home_rows, kv_heads, query_groups, HEAD_DIM_SIZE) + self_term
    )
    attention = (numerators / totals[:, :, :, None]).reshape(home_rows, -1).astype(jnp.bfloat16)
    head_terms = lax.dot_general(
        attention, output_matrix, (((1,), (1,)), ((), ())), preferred_element_type=jnp.float32
    )
    projected = lax.psum_scatter(head_terms, "feat", scatter_dimension=0, tiled=True)
    residual = stream.astype(jnp.float32) + normalize(projected, attention_gain)
    normed = normalize(residual, feedforward_gain).astype(jnp.bfloat16)
    hidden = activate(
        lax.all_gather(normed, ("page", "feat"), axis=0, tiled=True), gate_matrix, linear_matrix
    )
    feedforward = lax.psum_scatter(
        jnp.dot(hidden, down_matrix, preferred_element_type=jnp.float32),
        ("page", "feat"),
        scatter_dimension=0,
        tiled=True,
    )
    return (residual + normalize(feedforward, closing_gain)).astype(jnp.bfloat16)


def solution(mesh):
    placed = (
        P("page", "feat"),
        P("page", "feat"),
        P("page", "feat"),
        P("page", None, "feat"),
        P("page", None, "feat"),
        P(),
        P(),
        P(),
        P(("page", "feat"), None),
        P(None, "feat"),
        P(),
        P(),
        P(("page", "feat"), None),
        P(("page", "feat"), None),
        P(("page", "feat"), None),
        P(),
    )
    return jax.shard_map(
        per_device, mesh=mesh, in_specs=placed, out_specs=P(("page", "feat"), None), check_vma=False
    )
```

profile of v0, /device:TPU:2, one launch (start us, length us, event | category | flops | bytes accessed | tf_op | source)
XLA Modules:
  0.0 780.5 jit_solution(16183047905571098049)
XLA Ops:
  6.5 0.8 compare_select_fusion.3
  7.3 0.7 compare_and_fusion.1
  8.0 0.8 copy.32
  8.9 0.7 gather_fusion
  10.2 0.7 gather_fusion.1
  11.6 1.6 gather_fusion.3
  13.2 1.5 gather_fusion.4
  14.7 0.7 iota_add_fusion
  15.5 0.7 copy.34
  16.3 0.7 compare_and_fusion
  17.5 56.0 %all_gather.6 = bf16[256,512]{1,0:T(8,128)(2,1)} all-gather(bf16[8,512]{1,0:T(8,128)(2,1)S(1)} %copy-done.9), channel_id=1, replica_groups=mesh['page'=32,'feat'=8] {'page'}, dimensions={0}, use_global_device_ids=true | all-gather | bytes 270336 | tf_op jit(solution)/shard_map/all_gather | solution.py:60
  73.6 2.1 reshape.290
  75.6 2.5 reshape.291
  78.2 2.0 gather_fusion.2
  80.2 0.8 fusion.51
  81.0 3.0 fusion.74
  84.7 1.4 convolution_bitcast_fusion
  87.9 70.8 %all-reduce = f32[256,4]{0,1:T(4,128)S(1)} all-reduce(f32[256,4]{0,1:T(4,128)S(1)} %convolution_bitcast_fusion.1), channel_id=3, replica_groups=mesh['page'=32,'feat'=8] {'page'}, use_global_device_ids=true, to_apply=%region_5.6.clone | all-reduce | flops 1024 | bytes 8192
  158.8 141.3 %reduce-scatter.3.cloned.1.call-done = f32[8,512]{1,0:T(8,128)} async-done(((f32[256,512]{1,0:T(8,128)}), f32[8,512]{1,0:T(8,128)}) %reduce-scatter.3.cloned.1.call-update) | async-done | bytes 16400 | tf_op jit(solution)/shard_map/reduce_scatter | solution.py:111
  300.1 0.8 divide_convert_fusion
  300.9 4.3 fusion.75
  306.0 62.1 %all-reduce.6.cloned.1.call-done = f32[8,4608]{1,0:T(8,128)} async-done(((f32[8,4608]{1,0:T(8,128)}), f32[8,4608]{1,0:T(8,128)}) %all-reduce.6.cloned.1.call-update) | async-done | bytes 147472
  368.0 2.2 multiply_reduce_fusion.2
  371.0 2.2 multiply_reduce_fusion.1
  373.9 0.6 fusion.59
  374.6 114.9 %all-gather.3.cloned.1.call-done = bf16[256,1,4608]{2,1,0:T(2,128)(2,1)} async-done(((bf16[1,1,4608]{2,1,0:T(2,128)(2,1)}), bf16[256,1,4608]{2,1,0:T(2,128)(2,1)}) %all-gather.3.cloned.1.call-update) | async-done | bytes 2359312 | tf_op jit(solution)/shard_map/all_gather | solution.py:141
  489.5 3.7 fusion.46
  493.2 7.3 fusion.33
  500.5 0.7 copy-done.8
  501.2 269.0 %all-reduce.8.cloned.1.call-done = f32[256,4608]{1,0:T(8,128)} async-done(((f32[256,4608]{1,0:T(8,128)}), f32[256,4608]{1,0:T(8,128)}) %all-reduce.8.cloned.1.call-update) | async-done | bytes 4718608
  770.2 1.6 multiply_reduce_fusion
  772.4 1.6 fusion.57
  (70 shorter events, 4.9 us)
Async XLA Ops:
  6.5 486.6 %copy-start = (bf16[144,4608]{1,0:T(8,128)(2,1)S(1)}, bf16[144,4608]{1,0:T(8,128)(2,1)}, u32[]{:S(2)}) copy-start(bf16[144,4608]{1,0:T(8,128)(2,1)} %param.30) | copy-start | bytes 3981316
  6.5 3.6 copy-start.1
  6.5 293.6 %reduce-scatter.3.cloned.1.call-start = ((), (), s32[]{:S(2)}) async-start(), calls=%async_computation.1 | async-start | bytes 540672 | tf_op jit(solution)/shard_map/reduce_scatter | solution.py:111
  13.2 4.4 copy-start.9
  13.2 60.4 %copy-start.2 = (bf16[16,256,256]{2,1,0:T(8,128)(2,1)S(1)}, bf16[16,256,256]{2,1,0:T(8,128)(2,1)}, u32[]{:S(2)}) copy-start(bf16[16,256,256]{2,1,0:T(8,128)(2,1)} %param.19) | copy-start | bytes 6291460
  84.0 0.7 copy-start.12
  84.0 2.1 copy-start.4
  84.0 2.2 copy-start.10
  84.0 2.2 copy-start.13
  84.0 2.4 copy-start.15
  84.0 74.8 %copy-start.11 = (bf16[8,256]{1,0:T(8,128)(2,1)S(1)}, bf16[8,256]{1,0:T(8,128)(2,1)}, u32[]{:S(2)}) copy-start(bf16[8,256]{1,0:T(8,128)(2,1)} %param.18) | copy-start | bytes 12292
  86.1 282.0 %all-reduce.6.cloned.1.call-start = ((), (), s32[]{:S(2)}) async-start(), calls=%async_computation.3 | async-start | bytes 294912
  300.9 4.5 copy-start.14
  300.9 5.0 copy-start.6
  300.9 5.0 copy-start.7
  300.9 70.0 %copy-start.5 = (bf16[1,4608]{1,0:T(2,128)(2,1)S(1)}, bf16[1,4608]{1,0:T(2,128)(2,1)}, u32[]{:S(2)}) copy-start(bf16[1,4608]{1,0:T(2,128)(2,1)} %param.24) | copy-start | bytes 27652
  305.3 184.2 %all-gather.3.cloned.1.call-start = ((), (), s32[]{:S(2)}) async-start(), calls=%async_computation.2 | async-start | bytes 4737024 | tf_op jit(solution)/shard_map/all_gather | solution.py:141
  374.5 118.7 %copy-start.3 = (bf16[144,4608]{1,0:T(8,128)(2,1)S(1)}, bf16[144,4608]{1,0:T(8,128)(2,1)}, u32[]{:S(2)}) copy-start(bf16[144,4608]{1,0:T(8,128)(2,1)} %param.29) | copy-start | bytes 3981316
  374.5 395.7 %all-reduce.8.cloned.1.call-start = ((), (), s32[]{:S(2)}) async-start(), calls=%async_computation.4 | async-start | bytes 9437184
  500.5 0.7 copy-start.8
Sparse Core Ops, SparseCore 0:
  86.2 213.8 reduce-scatter.2
  305.4 62.5 all-reduce.5
  374.6 114.7 all-gather.2
  500.6 269.5 all-reduce.7
where the time goes:
time: 781 us
  waiting for transfers between devices  587 us (75%)
  blocking collectives  127 us (16%)
  matrix products  20.4 us (3%)
  between operations  16.1 us (2%)
  local copies, waits for them, and re-layouts  15.3 us (2%)
  other arithmetic  14.4 us (2%)
    unnamed x6, waiting for transfers between devices  331 us
    reduce_scatter x1, waiting for transfers between devices, per_device(): lax.psum_scatter(numerator_rows, 'page', scatter_dimension=0, tiled=True)  141 us
    all_gather x1, waiting for transfers between devices, per_device(): lax.all_gather(normed, ('page', 'feat'), axis=0, tiled=True)  115 us
    unnamed x1, blocking collectives  70.8 us
    all_gather x1, blocking collectives, per_device(): all_queries = lax.all_gather(queries, 'page', axis=0, tiled=True)  56 us
  transfers between devices with their start and end apart: 4, of which 4 were waited for; matrix products, arithmetic and copies ran while one was open for 0% of the time, Pallas kernels for 0%

commit v1 on v0

--- a/solution.py
+++ b/solution.py
@@ -3,12 +3,14 @@
 import jax
 import jax.numpy as jnp
 from jax import lax
-from jax.sharding import PartitionSpec as P
+from jax.sharding import Mesh, PartitionSpec as P
 
 HEAD_DIM_SIZE = 128
 QSCALAR = 144
 SOFTCAP = 50
 BEAMS = 8
+Z, X, Y, C = 8, 4, 4, 2
+PAGES = Z * X
 
 
 norm_eps = 1e-06
@@ -23,14 +25,12 @@
     return values * lax.rsqrt(mean_square + norm_eps) * gain_row.astype(jnp.float32)[None, :]
 
 
-def activate(segment, gate_matrix, linear_matrix):
-    gate_sums = lax.dot_general(
-        segment, gate_matrix, (((1,), (1,)), ((), ())), preferred_element_type=jnp.float32
-    )
-    lift_sums = lax.dot_general(
-        segment, linear_matrix, (((1,), (1,)), ((), ())), preferred_element_type=jnp.float32
-    )
-    return (jax.nn.gelu(gate_sums, approximate=True) * lift_sums).astype(jnp.bfloat16)
+def exchange(blocks, axes):
+    return lax.all_to_all(blocks, axes, 0, 0, tiled=True)
+
+
+def gather_blocks(block, axes, count):
+    return exchange(jnp.broadcast_to(block[None], (count,) + block.shape), axes)
 
 
 def per_device(
@@ -51,16 +51,22 @@
     down_matrix,
     closing_gain,
 ):
+    swap = [(0, 1), (1, 0)]
+    gate_other = lax.ppermute(gate_matrix, "c", swap)
+    linear_other = lax.ppermute(linear_matrix, "c", swap)
+    down_other = lax.ppermute(down_matrix, "c", swap)
+
     home_rows = queries.shape[0]
     slot_count = paged_keys.shape[0]
     page_len = paged_keys.shape[1]
     kv_heads = paged_keys.shape[2] // HEAD_DIM_SIZE
     query_groups = queries.shape[1] // HEAD_DIM_SIZE // kv_heads
     root_scale = math.sqrt(QSCALAR)
-    all_queries = lax.all_gather(queries, "page", axis=0, tiled=True)
+    page_id = lax.axis_index("z") * X + lax.axis_index("x")
+    all_queries = gather_blocks(queries, ("z", "x"), PAGES).reshape(-1, queries.shape[1])
     row_count = all_queries.shape[0]
     row_tables = jnp.take(block_tables, parents, axis=0)
-    slot_ids = lax.axis_index("page") * slot_count + jnp.arange(slot_count, dtype=jnp.int32)
+    slot_ids = page_id * slot_count + jnp.arange(slot_count, dtype=jnp.int32)
     matches = row_tables[None, :, :] == slot_ids[:, None, None]
     in_use = jnp.any(matches, axis=2)
     block_index = jnp.arange(row_tables.shape[1], dtype=jnp.int32)
@@ -95,22 +101,26 @@
         preferred_element_type=jnp.float32,
     )
     selector = (beam_rows[:, :, None] == row_ids[None, None, :]).astype(jnp.float32)
-    numerator_rows = jnp.einsum(
-        "avz,avo->zo",
-        selector,
-        slot_numerators.reshape(slot_count, BEAMS, -1),
-        precision=lax.Precision.HIGHEST,
+    payload = jnp.concatenate(
+        [
+            slot_numerators.reshape(slot_count, BEAMS, -1),
+            slot_totals.reshape(slot_count, BEAMS, -1),
+        ],
+        axis=2,
     )
-    total_rows = jnp.einsum(
-        "avz,avo->zo",
-        selector,
-        slot_totals.reshape(slot_count, BEAMS, -1),
-        precision=lax.Precision.HIGHEST,
+    rows_out = jnp.einsum("avz,avo->zo", selector, payload, precision=lax.Precision.HIGHEST)
+    width = queries.shape[1]
+    tops = rows_out[:, width:]
+    high = tops.astype(jnp.bfloat16)
+    low = (tops - high.astype(jnp.float32)).astype(jnp.bfloat16)
+    sent = jnp.concatenate(
+        [rows_out[:, :width].astype(jnp.bfloat16), high, low, jnp.zeros((row_count, 120), jnp.bfloat16)],
+        axis=1,
     )
-    home_numerators, home_totals = (
-        lax.psum_scatter(numerator_rows, "page", scatter_dimension=0, tiled=True),
-        lax.psum_scatter(total_rows, "page", scatter_dimension=0, tiled=True),
-    )
+    got = exchange(sent.reshape(PAGES, home_rows, width + 128), ("z", "x"))
+    summed = jnp.sum(got.astype(jnp.float32), axis=0)
+    home_numerators = summed[:, :width]
+    home_totals = summed[:, width : width + 4] + summed[:, width + 4 : width + 8]
     own_queries = queries.reshape(home_rows, kv_heads, query_groups, HEAD_DIM_SIZE)
     own_keys = fresh_token_keys.reshape(home_rows, kv_heads, HEAD_DIM_SIZE)
     own_values = fresh_token_values.reshape(home_rows, kv_heads, HEAD_DIM_SIZE)
@@ -133,41 +143,54 @@
     attention = (numerators / totals[:, :, :, None]).reshape(home_rows, -1).astype(jnp.bfloat16)
     head_terms = lax.dot_general(
         attention, output_matrix, (((1,), (1,)), ((), ())), preferred_element_type=jnp.float32
+    ).astype(jnp.bfloat16)
+    projected = jnp.sum(
+        exchange(head_terms, ("y", "c")).astype(jnp.float32), axis=0, keepdims=True
     )
-    projected = lax.psum_scatter(head_terms, "feat", scatter_dimension=0, tiled=True)
     residual = stream.astype(jnp.float32) + normalize(projected, attention_gain)
     normed = normalize(residual, feedforward_gain).astype(jnp.bfloat16)
-    hidden = activate(
-        lax.all_gather(normed, ("page", "feat"), axis=0, tiled=True), gate_matrix, linear_matrix
+    over_z = exchange(jnp.broadcast_to(normed, (Z, normed.shape[1])), "z")
+    segment = gather_blocks(over_z, ("x", "y"), X * Y).reshape(X * Y * Z, -1)
+
+    def dot_t(a, b):
+        return lax.dot_general(a, b, (((1,), (1,)), ((), ())), preferred_element_type=jnp.float32)
+
+    def part(gate, linear, down):
+        hidden = jax.nn.gelu(dot_t(segment, gate), approximate=True) * dot_t(segment, linear)
+        return jnp.dot(hidden.astype(jnp.bfloat16), down, preferred_element_type=jnp.float32)
+
+    terms = part(gate_matrix, linear_matrix, down_matrix) + part(
+        gate_other, linear_other, down_other
     )
-    feedforward = lax.psum_scatter(
-        jnp.dot(hidden, down_matrix, preferred_element_type=jnp.float32),
-        ("page", "feat"),
-        scatter_dimension=0,
-        tiled=True,
+    sent = terms.astype(jnp.bfloat16).reshape(X * Y, Z, -1)
+    over_xy = jnp.sum(exchange(sent, ("x", "y")).astype(jnp.float32), axis=0)
+    feedforward = jnp.sum(
+        exchange(over_xy.astype(jnp.bfloat16), "z").astype(jnp.float32), axis=0, keepdims=True
     )
     return (residual + normalize(feedforward, closing_gain)).astype(jnp.bfloat16)
 
 
 def solution(mesh):
+    torus = Mesh(mesh.devices.reshape(Z, X, Y, C), ("z", "x", "y", "c"))
+    page, feat, both = ("z", "x"), ("y", "c"), ("z", "x", "y", "c")
     placed = (
-        P("page", "feat"),
-        P("page", "feat"),
-        P("page", "feat"),
-        P("page", None, "feat"),
-        P("page", None, "feat"),
+        P(page, feat),
+        P(page, feat),
+        P(page, feat),
+        P(page, None, feat),
+        P(page, None, feat),
         P(),
         P(),
         P(),
-        P(("page", "feat"), None),
-        P(None, "feat"),
+        P(both, None),
+        P(None, feat),
         P(),
         P(),
-        P(("page", "feat"), None),
-        P(("page", "feat"), None),
-        P(("page", "feat"), None),
+        P(both, None),
+        P(both, None),
+        P(both, None),
         P(),
     )
     return jax.shard_map(
-        per_device, mesh=mesh, in_specs=placed, out_specs=P(("page", "feat"), None), check_vma=False
+        per_device, mesh=torus, in_specs=placed, out_specs=P(both, None), check_vma=False
     )

time: 781 us -> 154 us (0.20)
  waiting for transfers between devices: 587 us -> 32.5 us
  blocking collectives: 127 us -> 42.9 us
  starting transfers between devices: 0.13 us -> 31.4 us
  between operations: 16.1 us -> 2.62 us
    unnamed x6 -> x0, waiting for transfers between devices: 331 us -> none
    reduce_scatter x1 -> x0, waiting for transfers between devices: 141 us -> none  [per_device(): lax.psum_scatter(numerator_rows, 'page', scatter_dimension=0, tiled=True)]
    all_gather x1 -> x0, waiting for transfers between devices: 115 us -> none  [per_device(): lax.all_gather(normed, ('page', 'feat'), axis=0, tiled=True)]
    unnamed x1 -> x0, blocking collectives: 70.8 us -> none
    all_gather x1 -> x0, blocking collectives: 56 us -> none  [per_device(): all_queries = lax.all_gather(queries, 'page', axis=0, tiled=True)]
    all_to_all x0 -> x3, blocking collectives: none -> 42.9 us  [exchange(): return lax.all_to_all(blocks, axes, 0, 0, tiled=True)]
    all_to_all x0 -> x4, waiting for transfers between devices: none -> 32.5 us  [exchange(): return lax.all_to_all(blocks, axes, 0, 0, tiled=True)]
    all_to_all x0 -> x4, starting transfers between devices: none -> 30.8 us  [exchange(): return lax.all_to_all(blocks, axes, 0, 0, tiled=True)]
  transfers between devices with their start and end apart: 4 -> 7, of which waited for: 4 -> 3; matrix products, arithmetic and copies ran while one was open for 0% -> 13% of each run, Pallas kernels for 0% -> 0%
where the time goes in v1:
time: 154 us; the launch traced here: 153 us
  blocking collectives  42.9 us (28%)
  waiting for transfers between devices  32.5 us (21%)
  starting transfers between devices  31.4 us (20%)
  matrix products  18.5 us (12%)
  local copies, waits for them, and re-layouts  16.9 us (11%)
  other arithmetic  8.27 us (5%)
  between operations  2.62 us (2%)
    all_to_all x3, blocking collectives, exchange(): return lax.all_to_all(blocks, axes, 0, 0, tiled=True)  42.9 us
    all_to_all x4, waiting for transfers between devices, exchange(): return lax.all_to_all(blocks, axes, 0, 0, tiled=True)  32.5 us
    all_to_all x4, starting transfers between devices, exchange(): return lax.all_to_all(blocks, axes, 0, 0, tiled=True)  30.8 us
    dot_general x2, matrix products, part(): jnp.dot(hidden.astype(jnp.bfloat16), down, preferred_element_type=jnp.flo...  7.8 us
    dot_general x1, matrix products, per_device(): lax.dot_general(attention, output_matrix, (((1,), (1,)), ((), ())), prefe...  3.67 us
    dot_general x2, matrix products, dot_t(): lax.dot_general(a, b, (((1,), (1,)), ((), ())), preferred_element_type=jn...  3.62 us
  transfers between devices with their start and end apart: 7, of which 3 were waited for; matrix products, arithmetic and copies ran while one was open for 13% of the time, Pallas kernels for 0%

profile of v1, /device:TPU:2, one launch (start us, length us, event | category | flops | bytes accessed | tf_op | source)
XLA Modules:
  0.0 153.1 jit_solution(8012148412828250874)
XLA Ops:
  0.0 1.5 broadcast_in_dim.128
  1.5 11.6 %all-to-all-start = ((bf16[32,8,512]{2,1,0:T(8,128)(2,1)}), bf16[32,8,512]{2,1,0:T(8,128)(2,1)S(1)}, u32[]{:S(2)}, u32[]{:S(2)}) async-start(bf16[32,8,512]{2,1,0:T(8,128)(2,1)} %broadcast_in_dim.128), calls=%async_computation | async-start | bytes 524288 | tf_op jit(solution)/shard_map/all_to_all | solution.py:29
  13.1 0.7 compare_and_fusion.1
  14.5 0.8 copy.51
  15.3 0.7 gather_fusion
  17.5 1.6 %gather_fusion.3 = pred[128]{0:T(512)(128)(4,1)S(1)} fusion(pred[16,256]{1,0:T(8,128)(4,1)S(1)} %compare_reduce_fusion, s32[128]{0:T(128)S(1)} %reshape.364), kind=kCustom, calls=%fused_computation.3 | custom fusion | bytes 1280 | tf_op jit(solution)/shard_map/jit(take_along_axis)/gather | solution.py:78
  19.0 1.5 gather_fusion.4
  21.0 2.1 %reshape.326 = bf16[16,256,2,128]{3,2,1,0:T(2,128)(2,1)} reshape(bf16[16,256,256]{2,1,0:T(8,128)(2,1)S(1)} %copy-done.2) | data formatting | bytes 4194304 | tf_op jit(solution)/shard_map/reshape | solution.py:88
  23.1 2.5 %reshape.327 = bf16[16,256,2,128]{3,2,1,0:T(2,128)(2,1)S(1)} reshape(bf16[16,256,256]{2,1,0:T(8,128)(2,1)} %param.20) | data formatting | bytes 4194304 | tf_op jit(solution)/shard_map/reshape | solution.py:89
  25.9 0.8 gather_fusion.2
  26.8 2.4 %fusion.101 = (f32[16,8,2,2]{1,3,2,0:T(2,128)S(1)}, bf16[16,8,2,2,256]{4,1,3,2,0:T(8,128)(2,1)S(1)}) fusion(bf16[16,256,2,128,1]{3,2,1,0,4:T(2,128)(2,1)} %bitcast.84, bf16[16,8,2,2,128]{4,1,3,2,0:T(8,128)(2,1)S(1)} %bitcast.88, pred[16,8]{1,0:T(8,128)(4,1)S(1)} %get-tuple-element.11, pred[16,8,256]{2,1,0:T(8,128)(4,1)S(1)} %fusion.48), kind=kOutput, calls=%fused_computation.130 | convolution fusion | flops 34274816 | bytes 2525312 | tf_op jit(solution)/shard_map/sbkgd,stkd->sbkgt/dot_general | solution.py:90
  30.6 0.9 copy.59
  31.5 9.8 %all-to-all-start.1 = ((bf16[32,8,640]{2,1,0:T(8,128)(2,1)}), bf16[32,8,640]{2,1,0:T(8,128)(2,1)S(1)}, u32[]{:S(2)}, u32[]{:S(2)}) async-start(bf16[32,8,640]{2,1,0:T(8,128)(2,1)} %bitcast.10), calls=%async_computation.1 | async-start | bytes 655360 | tf_op jit(solution)/shard_map/all_to_all | solution.py:29
  41.5 11.8 %all-to-all-done.1 = bf16[32,8,640]{2,1,0:T(8,128)(2,1)S(1)} async-done(((bf16[32,8,640]{2,1,0:T(8,128)(2,1)}), bf16[32,8,640]{2,1,0:T(8,128)(2,1)S(1)}, u32[]{:S(2)}, u32[]{:S(2)}) %all-to-all-start.1) | async-done | bytes 327712 | tf_op jit(solution)/shard_map/all_to_all | solution.py:29
  53.7 3.7 %fusion.2 = bf16[8,1,4608]{2,0,1:T(8,128)(2,1)S(1)} fusion(bf16[8,512]{1,0:T(8,128)(2,1)S(1)} %bitcast.90, bf16[4608,512]{1,0:T(8,128)(2,1)} %param.25), kind=kOutput, calls=%fused_computation.9 | convolution fusion | flops 37785600 | bytes 4800512 | tf_op jit(solution)/shard_map/dot_general | solution.py:144
  58.0 0.7 reduce.8
  59.3 4.5 %all-to-all-start.2 = ((bf16[8,2,2304]{2,1,0:T(2,128)(2,1)}), bf16[8,2,2304]{2,1,0:T(2,128)(2,1)S(1)}, u32[]{:S(2)}, u32[]{:S(2)}) async-start(bf16[8,2,2304]{2,1,0:T(2,128)(2,1)} %reshape.389), calls=%async_computation.2 | async-start | bytes 147456 | tf_op jit(solution)/shard_map/all_to_all | solution.py:29
  63.8 5.6 %all-to-all-done.2 = bf16[8,2,2304]{2,1,0:T(2,128)(2,1)S(1)} async-done(((bf16[8,2,2304]{2,1,0:T(2,128)(2,1)}), bf16[8,2,2304]{2,1,0:T(2,128)(2,1)S(1)}, u32[]{:S(2)}, u32[]{:S(2)}) %all-to-all-start.2) | async-done | bytes 73760 | tf_op jit(solution)/shard_map/all_to_all | solution.py:29
  71.0 0.7 multiply_reduce_fusion.2
  72.6 1.1 reduce.9
  73.7 11.3 %all_to_all.44 = bf16[8,2,2304]{2,1,0:T(2,128)(2,1)S(1)} all-to-all(bf16[8,2,2304]{2,1,0:T(2,128)(2,1)S(1)} %reshape.391), channel_id=1, replica_groups=mesh['z'=8,'x'=4,'y'=4,'c'=2] {'z'}, dimensions={0} | all-to-all | bytes 147456 | tf_op jit(solution)/shard_map/all_to_all | solution.py:29
  85.1 1.1 broadcast_in_dim.136
  86.2 5.0 %all-to-all-start.4 = ((bf16[16,8,4608]{2,1,0:T(8,128)(2,1)}), bf16[16,8,4608]{2,1,0:T(8,128)(2,1)S(1)}, u32[]{:S(2)}, u32[]{:S(2)}) async-start(bf16[16,8,4608]{2,1,0:T(8,128)(2,1)} %broadcast_in_dim.136), calls=%async_computation.4 | async-start | bytes 2359296 | tf_op jit(solution)/shard_map/all_to_all | solution.py:29
  91.8 15.0 %all-to-all-done.4 = bf16[16,8,4608]{2,1,0:T(8,128)(2,1)S(1)} async-done(((bf16[16,8,4608]{2,1,0:T(8,128)(2,1)}), bf16[16,8,4608]{2,1,0:T(8,128)(2,1)S(1)}, u32[]{:S(2)}, u32[]{:S(2)}) %all-to-all-start.4) | async-done | bytes 1179680 | tf_op jit(solution)/shard_map/all_to_all | solution.py:29
  106.8 2.5 %fusion.56 = f32[128,144]{0,1:T(8,128)} fusion(bf16[144,4608]{1,0:T(8,128)(2,1)} %param.28, bf16[16,8,4608]{2,1,0:T(8,128)(2,1)S(1)} %all-to-all-done.4), kind=kOutput, calls=%fused_computation.57 | convolution fusion | flops 170016768 | bytes 2580480 | tf_op jit(solution)/shard_map/dot_general | solution.py:156
  109.3 1.1 fusion.25
  110.5 3.4 %fusion.40 = f32[128,4608]{1,0:T(8,128)S(1)} fusion(bf16[144,4608]{1,0:T(8,128)(2,1)} %param.30, f32[128,144]{0,1:T(8,128)} %fusion.56, bf16[144,4608]{1,0:T(8,128)(2,1)} %param.29, bf16[16,8,4608]{2,1,0:T(8,128)(2,1)S(1)} %all-to-all-done.4), kind=kOutput, calls=%fused_computation.31 | convolution fusion | flops 339775488 | bytes 6266880 | tf_op jit(solution)/shard_map/dot_general | solution.py:160
  113.9 4.4 %fusion.1 = bf16[16,8,4608]{2,1,0:T(8,128)(2,1)} fusion(f32[128,4608]{1,0:T(8,128)S(1)} %fusion.40, bf16[144,4608]{1,0:T(8,128)(2,1)} %collective-permute-done.2, f32[128,144]{0,1:T(8,128)} %fusion.25, bf16[144,4608]{1,0:T(8,128)(2,1)} %collective-permute-done, bf16[16,8,4608]{2,1,0:T(8,128)(2,1)S(1)} %all-to-all-done.4), kind=kOutput, calls=%fused_computation.7 | convolution fusion | flops 341102592 | bytes 7446528 | tf_op jit(solution)/shard_map/dot_general | solution.py:160
  118.3 20.7 %all_to_all.45 = bf16[16,8,4608]{2,1,0:T(8,128)(2,1)S(1)} all-to-all(bf16[16,8,4608]{2,1,0:T(8,128)(2,1)} %fusion.1), channel_id=1, replica_groups=mesh['z'=8,'x'=4,'y'=4,'c'=2] {'x','y'}, dimensions={0} | all-to-all | bytes 2359296 | tf_op jit(solution)/shard_map/all_to_all | solution.py:29
  139.2 0.7 reduce.10
  139.9 10.8 %all_to_all.46 = bf16[8,2,2304]{2,1,0:T(2,128)(2,1)S(1)} all-to-all(bf16[8,2,2304]{2,1,0:T(2,128)(2,1)S(1)} %reshape.393), channel_id=1, replica_groups=mesh['z'=8,'x'=4,'y'=4,'c'=2] {'z'}, dimensions={0} | all-to-all | bytes 147456 | tf_op jit(solution)/shard_map/all_to_all | solution.py:29
  151.0 0.7 multiply_reduce_fusion
  (89 shorter events, 8.7 us)
Async XLA Ops:
  0.0 41.3 %copy-start = (bf16[8,256]{1,0:T(8,128)(2,1)S(1)}, bf16[8,256]{1,0:T(8,128)(2,1)}, u32[]{:S(2)}) copy-start(bf16[8,256]{1,0:T(8,128)(2,1)} %param.17) | copy-start | bytes 12292
  0.0 16.6 %copy-start.1 = (s32[32]{0:T(128)S(1)}, s32[32]{0:T(128)}, u32[]{:S(2)}) copy-start(s32[32]{0:T(128)} %param.23) | copy-start | bytes 388
  1.5 24.4 %all-to-all-start = ((bf16[32,8,512]{2,1,0:T(8,128)(2,1)}), bf16[32,8,512]{2,1,0:T(8,128)(2,1)S(1)}, u32[]{:S(2)}, u32[]{:S(2)}) async-start(bf16[32,8,512]{2,1,0:T(8,128)(2,1)} %broadcast_in_dim.128), calls=%async_computation | async-start | bytes 524288 | tf_op jit(solution)/shard_map/all_to_all | solution.py:29
  19.0 1.9 %copy-start.2 = (bf16[16,256,256]{2,1,0:T(8,128)(2,1)S(1)}, bf16[16,256,256]{2,1,0:T(8,128)(2,1)}, u32[]{:S(2)}) copy-start(bf16[16,256,256]{2,1,0:T(8,128)(2,1)} %param.19) | copy-start | bytes 6291460
  30.4 10.9 %copy-start.9 = (bf16[8,512]{1,0:T(8,128)(2,1)S(1)}, bf16[8,512]{1,0:T(8,128)(2,1)}, u32[]{:S(2)}) copy-start(bf16[8,512]{1,0:T(8,128)(2,1)} %param.16) | copy-start | bytes 24580
  30.4 11.1 %copy-start.10 = (bf16[8,256]{1,0:T(8,128)(2,1)S(1)}, bf16[8,256]{1,0:T(8,128)(2,1)}, u32[]{:S(2)}) copy-start(bf16[8,256]{1,0:T(8,128)(2,1)} %param.18) | copy-start | bytes 12292
  31.5 21.8 %all-to-all-start.1 = ((bf16[32,8,640]{2,1,0:T(8,128)(2,1)}), bf16[32,8,640]{2,1,0:T(8,128)(2,1)S(1)}, u32[]{:S(2)}, u32[]{:S(2)}) async-start(bf16[32,8,640]{2,1,0:T(8,128)(2,1)} %bitcast.10), calls=%async_computation.1 | async-start | bytes 655360 | tf_op jit(solution)/shard_map/all_to_all | solution.py:29
  53.6 10.1 %copy-start.8 = (bf16[4608]{0:T(1024)(128)(2,1)S(1)}, bf16[4608]{0:T(1024)(128)(2,1)}, u32[]{:S(2)}) copy-start(bf16[4608]{0:T(1024)(128)(2,1)} %param.27) | copy-start | bytes 27652
  53.7 17.3 %copy-start.6 = (bf16[4608]{0:T(1024)(128)(2,1)S(1)}, bf16[4608]{0:T(1024)(128)(2,1)}, u32[]{:S(2)}) copy-start(bf16[4608]{0:T(1024)(128)(2,1)} %param.26) | copy-start | bytes 27652
  53.7 17.3 %copy-start.5 = (bf16[1,4608]{1,0:T(2,128)(2,1)S(1)}, bf16[1,4608]{1,0:T(2,128)(2,1)}, u32[]{:S(2)}) copy-start(bf16[1,4608]{1,0:T(2,128)(2,1)} %param.24) | copy-start | bytes 27652
  59.3 10.1 %all-to-all-start.2 = ((bf16[8,2,2304]{2,1,0:T(2,128)(2,1)}), bf16[8,2,2304]{2,1,0:T(2,128)(2,1)S(1)}, u32[]{:S(2)}, u32[]{:S(2)}) async-start(bf16[8,2,2304]{2,1,0:T(2,128)(2,1)} %reshape.389), calls=%async_computation.2 | async-start | bytes 147456 | tf_op jit(solution)/shard_map/all_to_all | solution.py:29
  71.7 0.7 copy-start.3
  86.2 20.6 %all-to-all-start.4 = ((bf16[16,8,4608]{2,1,0:T(8,128)(2,1)}), bf16[16,8,4608]{2,1,0:T(8,128)(2,1)S(1)}, u32[]{:S(2)}, u32[]{:S(2)}) async-start(bf16[16,8,4608]{2,1,0:T(8,128)(2,1)} %broadcast_in_dim.136), calls=%async_computation.4 | async-start | bytes 2359296 | tf_op jit(solution)/shard_map/all_to_all | solution.py:29
  91.2 18.1 %collective-permute-start.1 = (bf16[144,4608]{1,0:T(8,128)(2,1)}, bf16[144,4608]{1,0:T(8,128)(2,1)S(1)}, u32[]{:S(2)}, u32[]{:S(2)}) collective-permute-start(bf16[144,4608]{1,0:T(8,128)(2,1)} %param.29), channel_id=1, source_target_pairs={{0,1},{1,0},{2,3},{3,2},{4,5},{5,4},{6,7},{7,6},{8,9},{9,8},{10,11... | collective-permute-start | bytes 3981320 | tf_op jit(solution)/shard_map/ppermute | solution.py:56
  91.2 22.6 %collective-permute-start = (bf16[144,4608]{1,0:T(8,128)(2,1)}, bf16[144,4608]{1,0:T(8,128)(2,1)}, u32[]{:S(2)}, u32[]{:S(2)}) collective-permute-start(bf16[144,4608]{1,0:T(8,128)(2,1)} %param.28), channel_id=1, source_target_pairs={{0,1},{1,0},{2,3},{3,2},{4,5},{5,4},{6,7},{7,6},{8,9},{9,8},{10,11... | collective-permute-start | bytes 3981320 | tf_op jit(solution)/shard_map/ppermute | solution.py:55
  91.7 22.1 %collective-permute-start.2 = (bf16[144,4608]{1,0:T(8,128)(2,1)}, bf16[144,4608]{1,0:T(8,128)(2,1)}, u32[]{:S(2)}, u32[]{:S(2)}) collective-permute-start(bf16[144,4608]{1,0:T(8,128)(2,1)} %param.30), channel_id=1, source_target_pairs={{0,1},{1,0},{2,3},{3,2},{4,5},{5,4},{6,7},{7,6},{8,9},{9,8},{10,11... | collective-permute-start | bytes 3981320 | tf_op jit(solution)/shard_map/ppermute | solution.py:57
  139.0 13.4 %copy-start.7 = (bf16[4608]{0:T(1024)(128)(2,1)S(1)}, bf16[4608]{0:T(1024)(128)(2,1)}, u32[]{:S(2)}) copy-start(bf16[4608]{0:T(1024)(128)(2,1)} %param.31) | copy-start | bytes 27652
  139.0 13.4 %copy-start.4 = (f32[1,4608]{1,0:T(1,128)S(1)}, f32[1,4608]{1,0:T(1,128)}, u32[]{:S(2)}) copy-start(f32[1,4608]{1,0:T(1,128)} %copy-done.3) | copy-start | bytes 55300

commit v2 on v1

v2 whole, which is shorter than its diff:
```python
import jax
import jax.numpy as jnp
from jax import lax
from jax.experimental import pallas as pl
from jax.experimental.pallas import tpu as pltpu
from jax.sharding import Mesh, PartitionSpec as P

HEAD = 128
ROOT_SCALE = 12.0
SOFTCAP = 50.0
BEAMS = 8
Z, X, Y, C = 8, 4, 4, 2
PAGES = Z * X
D = 4608
FOLD = 640
SLOTS = 16
PAGE = 256
BF, F32 = jnp.bfloat16, jnp.float32

norm_eps = 1e-06


def kernel(body, outs, scratch=(), smem=0, n_in=0):
    specs = [pl.BlockSpec(memory_space=pltpu.SMEM)] * smem
    specs += [pl.BlockSpec(memory_space=pltpu.VMEM)] * (n_in - smem)
    return pl.pallas_call(
        body,
        out_shape=outs,
        in_specs=specs,
        out_specs=jax.tree.map(lambda _: pl.BlockSpec(memory_space=pltpu.VMEM), outs),
        scratch_shapes=list(scratch),
        name=body.__name__,
    )


def weight_of(raw):
    return jnp.exp(SOFTCAP * jnp.tanh(raw * (1.0 / (ROOT_SCALE * SOFTCAP))))


def dot_nt(a, b):
    return lax.dot_general(a, b, (((1,), (1,)), ((), ())), preferred_element_type=F32)


def attend(prompt, valid, q, k, v, out, acc, tacc):
    acc[...] = jnp.zeros_like(acc)
    tacc[...] = jnp.zeros_like(tacc)
    token = lax.broadcasted_iota(jnp.int32, (BEAMS, PAGE), 1)
    lane = lax.broadcasted_iota(jnp.int32, (BEAMS, HEAD), 1)
    for s in range(SLOTS):
        p = prompt[s]
        queries = q[p].astype(F32)
        live = token < valid[:, s : s + 1]
        live = jnp.concatenate([live, live], axis=0)
        sums = jnp.zeros((BEAMS, HEAD), F32)
        nums = []
        for h in range(2):
            pair = jnp.concatenate(
                [queries[:, (2 * h + g) * HEAD : (2 * h + g + 1) * HEAD] for g in range(2)], axis=0
            ).astype(BF)
            w = weight_of(dot_nt(pair, k[s, :, h * HEAD : (h + 1) * HEAD]))
            w = jnp.where(live, w, 0.0)
            t = jnp.sum(w, axis=1, keepdims=True)
            n = jnp.dot(w.astype(BF), v[s, :, h * HEAD : (h + 1) * HEAD], preferred_element_type=F32)
            for g in range(2):
                sums = jnp.where(lane % 4 == 2 * h + g, t[g * BEAMS : (g + 1) * BEAMS], sums)
                nums.append(n[g * BEAMS : (g + 1) * BEAMS])
        acc[p] += jnp.concatenate(nums, axis=1)
        tacc[p] += sums
    out[:, :, : 4 * HEAD] = acc[...].astype(BF)
    t = tacc[...]
    high = t.astype(BF).astype(F32)
    upper = lax.broadcasted_iota(jnp.int32, t.shape, 2) < 4
    out[:, :, 4 * HEAD :] = jnp.where(upper, high, t - high).astype(BF)


def fold_rows(parts, out, rows):
    for a in range(8):
        part = parts(a)
        for b in range(5):
            rows[pl.ds(64 * b + a, 8, stride=8), :] = part[:, b * HEAD : (b + 1) * HEAD]
    for r in range(8):
        for b in range(5):
            low = 64 * b + 8 * r
            out[r, :, b * HEAD : (b + 1) * HEAD] = rows[low : low + 8, :].astype(BF)


def project(got, q, fresh_k, fresh_v, wo, out, rows):
    total = got[0].astype(F32)
    for i in range(1, PAGES):
        total += got[i].astype(F32)
    heads = []
    for h in range(4):
        k = h // 2
        hs, ks = slice(h * HEAD, (h + 1) * HEAD), slice(k * HEAD, (k + 1) * HEAD)
        raw = jnp.sum(q[:, hs].astype(F32) * fresh_k[:, ks].astype(F32), axis=1, keepdims=True)
        own = weight_of(raw)
        base = 4 * HEAD + h
        denominator = total[:, base : base + 1] + total[:, base + 4 : base + 5] + own
        numerator = total[:, hs] + own.astype(BF).astype(F32) * fresh_v[:, ks].astype(F32)
        heads.append(numerator / denominator)
    attention = jnp.concatenate(heads, axis=1).astype(BF)

    def part(a):
        lo, hi = a * FOLD, min(D, (a + 1) * FOLD)
        terms = dot_nt(attention, wo[lo:hi, :])
        if hi - lo < FOLD:
            terms = jnp.concatenate([terms, jnp.zeros((8, FOLD - hi + lo), F32)], axis=1)
        return terms

    fold_rows(part, out, rows)


def total_of(got, count):
    total = got[0].astype(F32)
    for i in range(1, count):
        total += got[i].astype(F32)
    return total


def unit(v):
    square = jnp.sum(jnp.sum(v * v, axis=1, keepdims=True), axis=0, keepdims=True)
    return v * lax.rsqrt(square * (1.0 / D) + norm_eps)


def enter(got, stream, gain_a, gain_f, residual, spread):
    r = stream[...].astype(F32) + unit(total_of(got, Y * C)) * gain_a[...].astype(F32)
    residual[...] = r
    normed = (unit(r) * gain_f[...].astype(F32)).astype(BF)
    for i in range(Z):
        spread[i] = normed


def widen(got, out, rows):
    for z in range(Z):
        for b in range(5):
            low = 64 * b + 8 * z
            rows[low : low + 8, :] = got[z, :, b * HEAD : (b + 1) * HEAD].astype(F32)
    for t in range(D // HEAD):
        part = rows[pl.ds(64 * (t % 5) + t // 5, 8, stride=8), :].astype(BF)
        for i in range(X * Y):
            out[i, :, t * HEAD : (t + 1) * HEAD] = part


def feed(x, g0, l0, g1, l1, d0, d1, out):
    rows = x[...]

    def hidden(g, l):
        gate = dot_nt(rows, g[...])
        return (jax.nn.gelu(gate, approximate=True) * dot_nt(rows, l[...])).astype(BF)

    h0, h1 = hidden(g0, l0), hidden(g1, l1)
    step = 512
    for c in range(0, D, step):
        cut = slice(c, c + step)
        y = jnp.dot(h0, d0[:, cut], preferred_element_type=F32)
        y += jnp.dot(h1, d1[:, cut], preferred_element_type=F32)
        out[:, cut] = y.astype(BF)


def gather_sum(got, out, rows):
    def part(a):
        lo, hi = a * FOLD, min(D, (a + 1) * FOLD)
        total = got[0, :, lo:hi].astype(F32)
        for i in range(1, X * Y):
            total += got[i, :, lo:hi].astype(F32)
        if hi - lo < FOLD:
            total = jnp.concatenate([total, jnp.zeros((8, FOLD - hi + lo), F32)], axis=1)
        return total

    fold_rows(part, out, rows)


def leave(got, residual, gain, out):
    value = residual[...] + unit(total_of(got, Z)) * gain[...].astype(F32)
    for a in range(8):
        lo, hi = a * FOLD, min(D, (a + 1) * FOLD)
        out[:, lo:hi] = value[a : a + 1, : hi - lo].astype(BF)


def exchange(blocks, axes):
    return lax.all_to_all(blocks, axes, 0, 0, tiled=True)


def fold(v):
    return jnp.pad(v.reshape(-1), (0, 8 * FOLD - D)).reshape(8, FOLD)


def shaped(*shape, dtype=BF):
    return jax.ShapeDtypeStruct(shape, dtype)


def per_device(
    queries,
    fresh_token_keys,
    fresh_token_values,
    paged_keys,
    paged_values,
    block_tables,
    parents,
    prompt_lengths,
    stream,
    output_matrix,
    attention_gain,
    feedforward_gain,
    gate_matrix,
    linear_matrix,
    down_matrix,
    closing_gain,
):
    swap = [(0, 1), (1, 0)]
    gate_other = lax.ppermute(gate_matrix, "c", swap)
    linear_other = lax.ppermute(linear_matrix, "c", swap)
    down_other = lax.ppermute(down_matrix, "c", swap)

    all_queries = exchange(jnp.broadcast_to(queries[None], (PAGES,) + queries.shape), ("z", "x"))
    page_id = lax.axis_index("z") * X + lax.axis_index("x")
    slots = page_id * SLOTS + jnp.arange(SLOTS, dtype=jnp.int32)
    row_ids = jnp.arange(block_tables.shape[0], dtype=jnp.int32)
    lengths = jnp.repeat(prompt_lengths, BEAMS)
    first = PAGE * jnp.arange(block_tables.shape[1], dtype=jnp.int32)
    tokens = jnp.clip(lengths[:, None] - first[None, :], 0, PAGE)
    held = jnp.sum(
        jnp.where(block_tables[None] == slots[:, None, None], tokens[None], 0), axis=2
    )
    prompt = jnp.max(jnp.where(held > 0, (row_ids // BEAMS)[None], 0), axis=1)
    chosen = jnp.repeat(parents.reshape(-1, BEAMS), BEAMS, axis=0) == row_ids[:, None]
    valid = jnp.sum(jnp.where(chosen.T[:, None, :], held[None], 0), axis=2)

    sent = kernel(
        attend,
        shaped(PAGES, BEAMS, 5 * HEAD),
        [pltpu.VMEM((PAGES, BEAMS, 4 * HEAD), F32), pltpu.VMEM((PAGES, BEAMS, HEAD), F32)],
        1,
        5,
    )(prompt, valid, all_queries, paged_keys, paged_values)
    got = exchange(sent, ("z", "x"))
    rows = [pltpu.VMEM((5 * 64, HEAD), F32)]
    blocks = shaped(8, 8, FOLD)
    sent = kernel(project, blocks, rows, 0, 5)(
        got, queries, fresh_token_keys, fresh_token_values, output_matrix
    )
    got = exchange(sent, ("y", "c"))
    residual, sent = kernel(enter, (shaped(8, FOLD, dtype=F32), blocks), (), 0, 4)(
        got, fold(stream), fold(attention_gain), fold(feedforward_gain)
    )
    got = exchange(sent, "z")
    sent = kernel(widen, shaped(X * Y, Z, D), rows, 0, 1)(got)
    got = exchange(sent, ("x", "y")).reshape(X * Y * Z, D)
    sent = kernel(feed, shaped(X * Y * Z, D), (), 0, 7)(
        got, gate_matrix, linear_matrix, gate_other, linear_other, down_matrix, down_other
    )
    got = exchange(sent.reshape(X * Y, Z, D), ("x", "y"))
    sent = kernel(gather_sum, blocks, rows, 0, 1)(got)
    got = exchange(sent, "z")
    return kernel(leave, shaped(1, D), (), 0, 3)(got, residual, fold(closing_gain))


def solution(mesh):
    torus = Mesh(mesh.devices.reshape(Z, X, Y, C), ("z", "x", "y", "c"))
    page, feat, both = ("z", "x"), ("y", "c"), ("z", "x", "y", "c")
    placed = (
        P(page, feat),
        P(page, feat),
        P(page, feat),
        P(page, None, feat),
        P(page, None, feat),
        P(),
        P(),
        P(),
        P(both, None),
        P(None, feat),
        P(),
        P(),
        P(both, None),
        P(both, None),
        P(both, None),
        P(),
    )
    return jax.shard_map(
        per_device, mesh=torus, in_specs=placed, out_specs=P(both, None), check_vma=False
    )
```

time: 154 us -> 151 us (0.981)
  Pallas kernels: 0 us -> 27.6 us
  matrix products: 18.5 us -> 0 us
  waiting for transfers between devices: 32.5 us -> 45.2 us
  blocking collectives: 42.9 us -> 33.6 us
  local copies, waits for them, and re-layouts: 16.9 us -> 9.56 us
  other arithmetic: 8.27 us -> 2.48 us
  between operations: 2.62 us -> 0.18 us
    pallas_call x0 -> x7, Pallas kernels: none -> 27.6 us  [the longest x1 8.48 us: per_device(): kernel(attend, shaped(PAGES, BEAMS, 5 * HEAD), [pltpu.VMEM((PAGES, BEAMS,...]
    dot_general x9 -> x0, matrix products: 18.5 us -> none  [the longest x2 7.8 us: part(): jnp.dot(hidden.astype(jnp.bfloat16), down, preferred_element_type=jnp.flo...]
    all_to_all x4 -> x5, waiting for transfers between devices: 32.5 us -> 45.2 us  [exchange(): return lax.all_to_all(blocks, axes, 0, 0, tiled=True)]
    all_to_all x3 -> x2, blocking collectives: 42.9 us -> 33.6 us  [exchange(): return lax.all_to_all(blocks, axes, 0, 0, tiled=True)]
    gather x8 -> x0, local copies, waits for them, and re-layouts: 5.53 us -> none  [the longest x3 1.74 us: per_device(): row_in_use = jnp.take_along_axis(in_use, beam_rows, axis=1)]
    unnamed x30 -> x20, local copies, waits for them, and re-layouts: 1.76 us -> 3.76 us
    reshape x4 -> x7, local copies, waits for them, and re-layouts: 4.98 us -> 3.43 us  [the longest x4 2.49 us: fold(): return jnp.pad(v.reshape(-1), (0, 8 * FOLD - D)).reshape(8, FOLD)]
    all_to_all x4 -> x5, starting transfers between devices: 30.8 us -> 30.4 us  [exchange(): return lax.all_to_all(blocks, axes, 0, 0, tiled=True)]
  transfers between devices with their start and end apart: 7 -> 8, of which waited for: 3 -> 5; matrix products, arithmetic and copies ran while one was open for 13% -> 5% of each run, Pallas kernels for 0% -> 6%
where the time goes in v2:
time: 151 us; the launch traced here: 150 us
  waiting for transfers between devices  45.2 us (30%)
  blocking collectives  33.6 us (22%)
  starting transfers between devices  31.1 us (21%)
  Pallas kernels  27.6 us (18%)
  local copies, waits for them, and re-layouts  9.56 us (6%)
  other arithmetic  2.48 us (2%)
    all_to_all x5, waiting for transfers between devices, exchange(): return lax.all_to_all(blocks, axes, 0, 0, tiled=True)  45.2 us
    all_to_all x2, blocking collectives, exchange(): return lax.all_to_all(blocks, axes, 0, 0, tiled=True)  33.6 us
    all_to_all x5, starting transfers between devices, exchange(): return lax.all_to_all(blocks, axes, 0, 0, tiled=True)  30.4 us
    pallas_call x1, Pallas kernels, per_device(): kernel(attend, shaped(PAGES, BEAMS, 5 * HEAD), [pltpu.VMEM((PAGES, BEAMS,...  8.48 us
    pallas_call x1, Pallas kernels, per_device(): kernel(feed, shaped(X * Y * Z, D), (), 0, 7)  6.94 us
    pallas_call x1, Pallas kernels, per_device(): kernel(project, blocks, rows, 0, 5)  4.63 us
    unnamed x20, local copies, waits for them, and re-layouts  3.76 us
  transfers between devices with their start and end apart: 8, of which 5 were waited for; matrix products, arithmetic and copies ran while one was open for 5% of the time, Pallas kernels for 6%

profile of v2, /device:TPU:2, one launch (start us, length us, event | category | flops | bytes accessed | tf_op | source)
XLA Modules:
  0.0 149.7 jit_solution(9784122709807440393)
XLA Ops:
  0.0 1.4 broadcast_in_dim.70
  1.4 11.6 %all-to-all-start = ((bf16[32,8,512]{2,1,0:T(8,128)(2,1)}), bf16[32,8,512]{2,1,0:T(8,128)(2,1)S(1)}, u32[]{:S(2)}, u32[]{:S(2)}) async-start(bf16[32,8,512]{2,1,0:T(8,128)(2,1)} %broadcast_in_dim.70), calls=%async_computation | async-start | bytes 524288 | tf_op jit(solution)/shard_map/all_to_all | solution.py:181
  13.1 0.7 broadcast_in_dim.62
  14.0 0.8 select_reduce_fusion.1
  14.8 0.8 reshape.82
  15.9 0.7 select_reduce_fusion.2.prompt
  16.6 0.8 select_reduce_fusion.valid
  17.4 6.9 %all-to-all-done.q = bf16[32,8,512]{2,1,0:T(8,128)(2,1)S(1)} async-done(((bf16[32,8,512]{2,1,0:T(8,128)(2,1)}), bf16[32,8,512]{2,1,0:T(8,128)(2,1)S(1)}, u32[]{:S(2)}, u32[]{:S(2)}) %all-to-all-start) | async-done | bytes 262176 | tf_op jit(solution)/shard_map/all_to_all | solution.py:181
  24.3 0.7 copy-done.3
  25.0 8.5 %attend.1 = bf16[32,8,640]{2,1,0:T(8,128)(2,1)} custom-call(s32[16]{0:T(128)} %select_reduce_fusion.2.prompt, s32[8,16]{1,0:T(8,128)} %select_reduce_fusion.valid, bf16[32,8,512]{2,1,0:T(8,128)(2,1)} %copy-done.3, bf16[16,256,256]{2,1,0:T(8,128)(2,1)} %k.1, bf16[16,256,256]{2,1,0:T(8,128)(2,1)} %v.1), custom_call_target="tpu_custom_call" | custom-call | tf_op jit(solution)/shard_map/attend/pallas_call | solution.py:229
  33.4 5.6 %all-to-all-start.1 = ((bf16[32,8,640]{2,1,0:T(8,128)(2,1)}), bf16[32,8,640]{2,1,0:T(8,128)(2,1)S(1)}, u32[]{:S(2)}, u32[]{:S(2)}) async-start(bf16[32,8,640]{2,1,0:T(8,128)(2,1)} %attend.1), calls=%async_computation.1 | async-start | bytes 655360 | tf_op jit(solution)/shard_map/all_to_all | solution.py:181
  39.8 11.1 %all-to-all-done.1.got = bf16[32,8,640]{2,1,0:T(8,128)(2,1)S(1)} async-done(((bf16[32,8,640]{2,1,0:T(8,128)(2,1)}), bf16[32,8,640]{2,1,0:T(8,128)(2,1)S(1)}, u32[]{:S(2)}, u32[]{:S(2)}) %all-to-all-start.1) | async-done | bytes 327712 | tf_op jit(solution)/shard_map/all_to_all | solution.py:181
  50.9 0.7 copy-done.2
  51.6 4.6 %project.1 = bf16[8,8,640]{2,1,0:T(8,128)(2,1)} custom-call(bf16[32,8,640]{2,1,0:T(8,128)(2,1)} %copy-done.2, bf16[8,512]{1,0:T(8,128)(2,1)} %q.1, bf16[8,256]{1,0:T(8,128)(2,1)} %fresh_k.1, bf16[8,256]{1,0:T(8,128)(2,1)} %fresh_v.1, bf16[4608,512]{1,0:T(8,128)(2,1)} %wo.1), custom_call_target="tpu_custom_call" | custom-call | tf_op jit(solution)/shard_map/project/pallas_call | solution.py:239
  56.2 4.5 %all-to-all-start.2 = ((bf16[8,8,640]{2,1,0:T(8,128)(2,1)}), bf16[8,8,640]{2,1,0:T(8,128)(2,1)S(1)}, u32[]{:S(2)}, u32[]{:S(2)}) async-start(bf16[8,8,640]{2,1,0:T(8,128)(2,1)} %project.1), calls=%async_computation.2 | async-start | bytes 163840 | tf_op jit(solution)/shard_map/all_to_all | solution.py:181
  60.8 0.6 reshape.85.stream
  62.6 3.7 %all-to-all-done.2.got = bf16[8,8,640]{2,1,0:T(8,128)(2,1)S(1)} async-done(((bf16[8,8,640]{2,1,0:T(8,128)(2,1)}), bf16[8,8,640]{2,1,0:T(8,128)(2,1)S(1)}, u32[]{:S(2)}, u32[]{:S(2)}) %all-to-all-start.2) | async-done | bytes 81952 | tf_op jit(solution)/shard_map/all_to_all | solution.py:181
  66.4 0.6 copy-done.4
  67.0 1.8 %enter.1 = (f32[8,640]{1,0:T(8,128)}, bf16[8,8,640]{2,1,0:T(8,128)(2,1)}) custom-call(bf16[8,8,640]{2,1,0:T(8,128)(2,1)} %copy-done.4, bf16[8,640]{1,0:T(8,128)(2,1)} %reshape.85.stream, bf16[8,640]{1,0:T(8,128)(2,1)} %reshape.86.gain_a, bf16[8,640]{1,0:T(8,128)(2,1)} %reshape.87.gain_f), custom_call_target="tpu_custom_call" | custom-call | tf_op jit(solution)/shard_map/enter/pallas_call | solution.py:243
  68.8 12.5 %all_to_all.35.got = bf16[8,8,640]{2,1,0:T(8,128)(2,1)} all-to-all(bf16[8,8,640]{2,1,0:T(8,128)(2,1)} %get-tuple-element.7), channel_id=1, replica_groups=mesh['z'=8,'x'=4,'y'=4,'c'=2] {'z'}, dimensions={0} | all-to-all | bytes 163840 | tf_op jit(solution)/shard_map/all_to_all | solution.py:181
  81.3 2.1 %widen.1 = bf16[16,8,4608]{2,1,0:T(8,128)(2,1)} custom-call(bf16[8,8,640]{2,1,0:T(8,128)(2,1)} %all_to_all.35.got), custom_call_target="tpu_custom_call" | custom-call | tf_op jit(solution)/shard_map/widen/pallas_call | solution.py:247
  83.4 5.4 %all-to-all-start.4 = ((bf16[16,8,4608]{2,1,0:T(8,128)(2,1)}), bf16[16,8,4608]{2,1,0:T(8,128)(2,1)S(1)}, u32[]{:S(2)}, u32[]{:S(2)}) async-start(bf16[16,8,4608]{2,1,0:T(8,128)(2,1)} %widen.1), calls=%async_computation.4 | async-start | bytes 2359296 | tf_op jit(solution)/shard_map/all_to_all | solution.py:181
  88.8 15.6 %all-to-all-done.4 = bf16[16,8,4608]{2,1,0:T(8,128)(2,1)S(1)} async-done(((bf16[16,8,4608]{2,1,0:T(8,128)(2,1)}), bf16[16,8,4608]{2,1,0:T(8,128)(2,1)S(1)}, u32[]{:S(2)}, u32[]{:S(2)}) %all-to-all-start.4) | async-done | bytes 1179680 | tf_op jit(solution)/shard_map/all_to_all | solution.py:181
  104.5 1.1 copy-done
  105.5 6.9 %feed.1 = bf16[128,4608]{1,0:T(8,128)(2,1)} custom-call(bf16[128,4608]{1,0:T(8,128)(2,1)} %bitcast.6, bf16[144,4608]{1,0:T(8,128)(2,1)} %g0.1, bf16[144,4608]{1,0:T(8,128)(2,1)} %l0.1, bf16[144,4608]{1,0:T(8,128)(2,1)} %collective-permute-done.g1, bf16[144,4608]{1,0:T(8,128)(2,1)} %collective-permute-done.1.l1, bf16[144,4608]{1,0:T(8,128)(2,1)} %d0.1, ...), custom_call_target="tpu_custom_call" | custom-call | tf_op jit(solution)/shard_map/feed/pallas_call | solution.py:249
  112.4 21.1 %all_to_all.36.got = bf16[16,8,4608]{2,1,0:T(8,128)(2,1)} all-to-all(bf16[16,8,4608]{2,1,0:T(8,128)(2,1)} %bitcast.7), channel_id=1, replica_groups=mesh['z'=8,'x'=4,'y'=4,'c'=2] {'x','y'}, dimensions={0} | all-to-all | bytes 2359296 | tf_op jit(solution)/shard_map/all_to_all | solution.py:181
  133.6 2.1 %gather_sum.1 = bf16[8,8,640]{2,1,0:T(8,128)(2,1)} custom-call(bf16[16,8,4608]{2,1,0:T(8,128)(2,1)} %all_to_all.36.got), custom_call_target="tpu_custom_call" | custom-call | tf_op jit(solution)/shard_map/gather_sum/pallas_call | solution.py:253
  135.7 3.4 %all-to-all-start.6 = ((bf16[8,8,640]{2,1,0:T(8,128)(2,1)}), bf16[8,8,640]{2,1,0:T(8,128)(2,1)S(1)}, u32[]{:S(2)}, u32[]{:S(2)}) async-start(bf16[8,8,640]{2,1,0:T(8,128)(2,1)} %gather_sum.1), calls=%async_computation.6 | async-start | bytes 163840 | tf_op jit(solution)/shard_map/all_to_all | solution.py:181
  139.0 0.6 reshape.90.gain
  139.7 7.8 %all-to-all-done.6.got = bf16[8,8,640]{2,1,0:T(8,128)(2,1)S(1)} async-done(((bf16[8,8,640]{2,1,0:T(8,128)(2,1)}), bf16[8,8,640]{2,1,0:T(8,128)(2,1)S(1)}, u32[]{:S(2)}, u32[]{:S(2)}) %all-to-all-start.6) | async-done | bytes 81952 | tf_op jit(solution)/shard_map/all_to_all | solution.py:181
  147.5 0.6 copy-done.5
  148.1 1.6 %leave.1 = bf16[1,4608]{1,0:T(2,128)(2,1)} custom-call(bf16[8,8,640]{2,1,0:T(8,128)(2,1)} %copy-done.5, f32[8,640]{1,0:T(8,128)} %get-tuple-element.8.residual, bf16[8,640]{1,0:T(8,128)(2,1)} %reshape.90.gain), custom_call_target="tpu_custom_call" | custom-call | tf_op jit(solution)/shard_map/leave/pallas_call | solution.py:255
  (37 shorter events, 2.5 us)
Async XLA Ops:
  1.4 22.8 %all-to-all-start = ((bf16[32,8,512]{2,1,0:T(8,128)(2,1)}), bf16[32,8,512]{2,1,0:T(8,128)(2,1)S(1)}, u32[]{:S(2)}, u32[]{:S(2)}) async-start(bf16[32,8,512]{2,1,0:T(8,128)(2,1)} %broadcast_in_dim.70), calls=%async_computation | async-start | bytes 524288 | tf_op jit(solution)/shard_map/all_to_all | solution.py:181
  17.4 21.6 %copy-start.1 = (bf16[144,4608]{1,0:T(8,128)(2,1)S(1)}, bf16[144,4608]{1,0:T(8,128)(2,1)}, u32[]{:S(2)}) copy-start(bf16[144,4608]{1,0:T(8,128)(2,1)} %g0.1) | copy-start | bytes 3981316
  24.3 0.7 copy-start.3
  33.4 17.4 %all-to-all-start.1 = ((bf16[32,8,640]{2,1,0:T(8,128)(2,1)}), bf16[32,8,640]{2,1,0:T(8,128)(2,1)S(1)}, u32[]{:S(2)}, u32[]{:S(2)}) async-start(bf16[32,8,640]{2,1,0:T(8,128)(2,1)} %attend.1), calls=%async_computation.1 | async-start | bytes 655360 | tf_op jit(solution)/shard_map/all_to_all | solution.py:181
  39.0 21.7 %copy-start.6 = (bf16[1,4608]{1,0:T(2,128)(2,1)S(1)}, bf16[1,4608]{1,0:T(2,128)(2,1)}, u32[]{:S(2)}) copy-start(bf16[1,4608]{1,0:T(2,128)(2,1)} %param.24) | copy-start | bytes 27652
  39.0 22.4 %copy-start.7 = (bf16[4608]{0:T(1024)(128)(2,1)S(1)}, bf16[4608]{0:T(1024)(128)(2,1)}, u32[]{:S(2)}) copy-start(bf16[4608]{0:T(1024)(128)(2,1)} %param.26) | copy-start | bytes 27652
  39.0 23.0 %copy-start.8 = (bf16[4608]{0:T(1024)(128)(2,1)S(1)}, bf16[4608]{0:T(1024)(128)(2,1)}, u32[]{:S(2)}) copy-start(bf16[4608]{0:T(1024)(128)(2,1)} %param.27) | copy-start | bytes 27652
  39.1 49.7 %collective-permute-start = (bf16[144,4608]{1,0:T(8,128)(2,1)S(1)}, bf16[144,4608]{1,0:T(8,128)(2,1)}, u32[]{:S(2)}, u32[]{:S(2)}) collective-permute-start(bf16[144,4608]{1,0:T(8,128)(2,1)S(1)} %copy-done.1), channel_id=1, source_target_pairs={{0,1},{1,0},{2,3},{3,2},{4,5},{5,4},{6,7},{7,6},{8,9},{9,8},{10,11... | collective-permute-start | bytes 3981320 | tf_op jit(solution)/shard_map/ppermute | solution.py:211
  39.2 49.6 %collective-permute-start.1 = (bf16[144,4608]{1,0:T(8,128)(2,1)}, bf16[144,4608]{1,0:T(8,128)(2,1)}, u32[]{:S(2)}, u32[]{:S(2)}) collective-permute-start(bf16[144,4608]{1,0:T(8,128)(2,1)} %l0.1), channel_id=1, source_target_pairs={{0,1},{1,0},{2,3},{3,2},{4,5},{5,4},{6,7},{7,6},{8,9},{9,8},{10,11... | collective-permute-start | bytes 3981320 | tf_op jit(solution)/shard_map/ppermute | solution.py:212
  39.7 49.2 %collective-permute-start.2 = (bf16[144,4608]{1,0:T(8,128)(2,1)}, bf16[144,4608]{1,0:T(8,128)(2,1)}, u32[]{:S(2)}, u32[]{:S(2)}) collective-permute-start(bf16[144,4608]{1,0:T(8,128)(2,1)} %d0.1), channel_id=1, source_target_pairs={{0,1},{1,0},{2,3},{3,2},{4,5},{5,4},{6,7},{7,6},{8,9},{9,8},{10,11... | collective-permute-start | bytes 3981320 | tf_op jit(solution)/shard_map/ppermute | solution.py:213
  50.9 0.7 copy-start.2
  56.2 10.2 %all-to-all-start.2 = ((bf16[8,8,640]{2,1,0:T(8,128)(2,1)}), bf16[8,8,640]{2,1,0:T(8,128)(2,1)S(1)}, u32[]{:S(2)}, u32[]{:S(2)}) async-start(bf16[8,8,640]{2,1,0:T(8,128)(2,1)} %project.1), calls=%async_computation.2 | async-start | bytes 163840 | tf_op jit(solution)/shard_map/all_to_all | solution.py:181
  66.4 0.6 copy-start.4
  83.4 21.1 %all-to-all-start.4 = ((bf16[16,8,4608]{2,1,0:T(8,128)(2,1)}), bf16[16,8,4608]{2,1,0:T(8,128)(2,1)S(1)}, u32[]{:S(2)}, u32[]{:S(2)}) async-start(bf16[16,8,4608]{2,1,0:T(8,128)(2,1)} %widen.1), calls=%async_computation.4 | async-start | bytes 2359296 | tf_op jit(solution)/shard_map/all_to_all | solution.py:181
  104.4 1.1 copy-start
  112.4 26.6 %copy-start.9 = (bf16[4608]{0:T(1024)(128)(2,1)S(1)}, bf16[4608]{0:T(1024)(128)(2,1)}, u32[]{:S(2)}) copy-start(bf16[4608]{0:T(1024)(128)(2,1)} %param.31) | copy-start | bytes 27652
  135.7 11.8 %all-to-all-start.6 = ((bf16[8,8,640]{2,1,0:T(8,128)(2,1)}), bf16[8,8,640]{2,1,0:T(8,128)(2,1)S(1)}, u32[]{:S(2)}, u32[]{:S(2)}) async-start(bf16[8,8,640]{2,1,0:T(8,128)(2,1)} %gather_sum.1), calls=%async_computation.6 | async-start | bytes 163840 | tf_op jit(solution)/shard_map/all_to_all | solution.py:181
  147.5 0.6 copy-start.5

commit v3 on v2

--- a/solution.py
+++ b/solution.py
@@ -15,21 +15,22 @@
 FOLD = 640
 SLOTS = 16
 PAGE = 256
+BATCH = 4
 BF, F32 = jnp.bfloat16, jnp.float32
+VMEM, SMEM, HBM = pltpu.VMEM, pltpu.SMEM, pltpu.HBM
 
 norm_eps = 1e-06
 
 
-def kernel(body, outs, scratch=(), smem=0, n_in=0):
-    specs = [pl.BlockSpec(memory_space=pltpu.SMEM)] * smem
-    specs += [pl.BlockSpec(memory_space=pltpu.VMEM)] * (n_in - smem)
+def kernel(body, outs, spaces, scratch=(), mib=4):
     return pl.pallas_call(
         body,
         out_shape=outs,
-        in_specs=specs,
-        out_specs=jax.tree.map(lambda _: pl.BlockSpec(memory_space=pltpu.VMEM), outs),
+        in_specs=[pl.BlockSpec(memory_space=m) for m in spaces],
+        out_specs=jax.tree.map(lambda _: pl.BlockSpec(memory_space=VMEM), outs),
         scratch_shapes=list(scratch),
         name=body.__name__,
+        compiler_params=pltpu.CompilerParams(vmem_limit_bytes=mib << 20),
     )
 
 
@@ -41,31 +42,45 @@
     return lax.dot_general(a, b, (((1,), (1,)), ((), ())), preferred_element_type=F32)
 
 
-def attend(prompt, valid, q, k, v, out, acc, tacc):
+def attend(prompt, valid, q, k_hbm, v_hbm, out, k, v, acc, tacc, k_sem, v_sem):
+    def fetch(n, hbm, buf, sem):
+        some = pl.ds(n * BATCH, BATCH)
+        return pltpu.make_async_copy(hbm.at[some], buf.at[some], sem.at[n])
+
+    for n in range(SLOTS // BATCH):
+        fetch(n, k_hbm, k, k_sem).start()
+        fetch(n, v_hbm, v, v_sem).start()
     acc[...] = jnp.zeros_like(acc)
     tacc[...] = jnp.zeros_like(tacc)
     token = lax.broadcasted_iota(jnp.int32, (BEAMS, PAGE), 1)
-    lane = lax.broadcasted_iota(jnp.int32, (BEAMS, HEAD), 1)
-    for s in range(SLOTS):
-        p = prompt[s]
-        queries = q[p].astype(F32)
-        live = token < valid[:, s : s + 1]
-        live = jnp.concatenate([live, live], axis=0)
-        sums = jnp.zeros((BEAMS, HEAD), F32)
-        nums = []
-        for h in range(2):
-            pair = jnp.concatenate(
-                [queries[:, (2 * h + g) * HEAD : (2 * h + g + 1) * HEAD] for g in range(2)], axis=0
-            ).astype(BF)
-            w = weight_of(dot_nt(pair, k[s, :, h * HEAD : (h + 1) * HEAD]))
-            w = jnp.where(live, w, 0.0)
-            t = jnp.sum(w, axis=1, keepdims=True)
-            n = jnp.dot(w.astype(BF), v[s, :, h * HEAD : (h + 1) * HEAD], preferred_element_type=F32)
-            for g in range(2):
-                sums = jnp.where(lane % 4 == 2 * h + g, t[g * BEAMS : (g + 1) * BEAMS], sums)
-                nums.append(n[g * BEAMS : (g + 1) * BEAMS])
-        acc[p] += jnp.concatenate(nums, axis=1)
-        tacc[p] += sums
+    lane = lax.broadcasted_iota(jnp.int32, (BEAMS, HEAD), 1) % 4
+    blank = jnp.zeros((2 * BEAMS, HEAD), F32)
+    for n in range(SLOTS // BATCH):
+        slots = range(n * BATCH, (n + 1) * BATCH)
+        fetch(n, k_hbm, k, k_sem).wait()
+        scores, live = [], []
+        for s in slots:
+            queries = q[prompt[s]].astype(F32)
+            heads = [queries[:, i * HEAD : (i + 1) * HEAD] for i in range(4)]
+            left = jnp.concatenate([heads[0], heads[1], blank], axis=0)
+            right = jnp.concatenate([blank, heads[2], heads[3]], axis=0)
+            scores.append(dot_nt(jnp.concatenate([left, right], axis=1).astype(BF), k[s]))
+            live += [token < valid[:, s : s + 1]] * 4
+        w = weight_of(jnp.concatenate(scores, axis=0))
+        w = jnp.where(jnp.concatenate(live, axis=0), w, 0.0)
+        t = jnp.sum(w, axis=1, keepdims=True)
+        wb = w.astype(BF)
+        fetch(n, v_hbm, v, v_sem).wait()
+        for i, s in enumerate(slots):
+            p = prompt[s]
+            m = jnp.dot(wb[32 * i : 32 * i + 32], v[s], preferred_element_type=F32)
+            acc[p] += jnp.concatenate(
+                [m[0:8, :HEAD], m[8:16, :HEAD], m[16:24, HEAD:], m[24:32, HEAD:]], axis=1
+            )
+            sums = jnp.zeros((BEAMS, HEAD), F32)
+            for j in range(4):
+                sums = jnp.where(lane == j, t[32 * i + 8 * j : 32 * i + 8 * j + 8], sums)
+            tacc[p] += sums
     out[:, :, : 4 * HEAD] = acc[...].astype(BF)
     t = tacc[...]
     high = t.astype(BF).astype(F32)
@@ -122,10 +137,10 @@
     return v * lax.rsqrt(square * (1.0 / D) + norm_eps)
 
 
-def enter(got, stream, gain_a, gain_f, residual, spread):
-    r = stream[...].astype(F32) + unit(total_of(got, Y * C)) * gain_a[...].astype(F32)
+def enter(got, vectors, residual, spread):
+    r = vectors[0].astype(F32) + unit(total_of(got, Y * C)) * vectors[1].astype(F32)
     residual[...] = r
-    normed = (unit(r) * gain_f[...].astype(F32)).astype(BF)
+    normed = (unit(r) * vectors[2].astype(F32)).astype(BF)
     for i in range(Z):
         spread[i] = normed
 
@@ -141,7 +156,9 @@
             out[i, :, t * HEAD : (t + 1) * HEAD] = part
 
 
-def feed(x, g0, l0, g1, l1, d0, d1, out):
+def feed(x, g0, l0, g1, l1, d0, d1_hbm, out, d1, sem):
+    late = pltpu.make_async_copy(d1_hbm, d1, sem)
+    late.start()
     rows = x[...]
 
     def hidden(g, l):
@@ -149,6 +166,7 @@
         return (jax.nn.gelu(gate, approximate=True) * dot_nt(rows, l[...])).astype(BF)
 
     h0, h1 = hidden(g0, l0), hidden(g1, l1)
+    late.wait()
     step = 512
     for c in range(0, D, step):
         cut = slice(c, c + step)
@@ -170,8 +188,8 @@
     fold_rows(part, out, rows)
 
 
-def leave(got, residual, gain, out):
-    value = residual[...] + unit(total_of(got, Z)) * gain[...].astype(F32)
+def leave(got, residual, vectors, out):
+    value = residual[...] + unit(total_of(got, Z)) * vectors[3].astype(F32)
     for a in range(8):
         lo, hi = a * FOLD, min(D, (a + 1) * FOLD)
         out[:, lo:hi] = value[a : a + 1, : hi - lo].astype(BF)
@@ -181,8 +199,8 @@
     return lax.all_to_all(blocks, axes, 0, 0, tiled=True)
 
 
-def fold(v):
-    return jnp.pad(v.reshape(-1), (0, 8 * FOLD - D)).reshape(8, FOLD)
+def stay(v):
+    return pltpu.with_memory_space_constraint(v, HBM)
 
 
 def shaped(*shape, dtype=BF):
@@ -226,33 +244,52 @@
     chosen = jnp.repeat(parents.reshape(-1, BEAMS), BEAMS, axis=0) == row_ids[:, None]
     valid = jnp.sum(jnp.where(chosen.T[:, None, :], held[None], 0), axis=2)
 
+    vectors = jnp.stack([stream[0], attention_gain, feedforward_gain, closing_gain])
+    vectors = jnp.pad(vectors, ((0, 0), (0, 8 * FOLD - D))).reshape(4, 8, FOLD)
+    all_queries, vectors = lax.optimization_barrier((all_queries, vectors))
+
+    pages = pltpu.VMEM(paged_keys.shape, BF)
+    batches = pltpu.SemaphoreType.DMA((SLOTS // BATCH,))
     sent = kernel(
         attend,
         shaped(PAGES, BEAMS, 5 * HEAD),
-        [pltpu.VMEM((PAGES, BEAMS, 4 * HEAD), F32), pltpu.VMEM((PAGES, BEAMS, HEAD), F32)],
-        1,
-        5,
-    )(prompt, valid, all_queries, paged_keys, paged_values)
+        (SMEM, VMEM, VMEM, HBM, HBM),
+        [
+            pages,
+            pages,
+            pltpu.VMEM((PAGES, BEAMS, 4 * HEAD), F32),
+            pltpu.VMEM((PAGES, BEAMS, HEAD), F32),
+            batches,
+            batches,
+        ],
+        8,
+    )(prompt, valid, all_queries, stay(paged_keys), stay(paged_values))
     got = exchange(sent, ("z", "x"))
     rows = [pltpu.VMEM((5 * 64, HEAD), F32)]
     blocks = shaped(8, 8, FOLD)
-    sent = kernel(project, blocks, rows, 0, 5)(
-        got, queries, fresh_token_keys, fresh_token_values, output_matrix
+    sent = kernel(
+        project,
+        blocks,
+        (VMEM,) * 5,
+        rows,
+        8,
+    )(got, queries, fresh_token_keys, fresh_token_values, output_matrix)
+    sent, gate_other, linear_other, down_other = lax.optimization_barrier(
+        (sent, gate_other, linear_other, down_other)
     )
     got = exchange(sent, ("y", "c"))
-    residual, sent = kernel(enter, (shaped(8, FOLD, dtype=F32), blocks), (), 0, 4)(
-        got, fold(stream), fold(attention_gain), fold(feedforward_gain)
-    )
+    residual, sent = kernel(enter, (shaped(8, FOLD, dtype=F32), blocks), (VMEM,) * 2)(got, vectors)
     got = exchange(sent, "z")
-    sent = kernel(widen, shaped(X * Y, Z, D), rows, 0, 1)(got)
+    sent = kernel(widen, shaped(X * Y, Z, D), (VMEM,), rows)(got)
     got = exchange(sent, ("x", "y")).reshape(X * Y * Z, D)
-    sent = kernel(feed, shaped(X * Y * Z, D), (), 0, 7)(
+    late = [pltpu.VMEM(down_matrix.shape, BF), pltpu.SemaphoreType.DMA(())]
+    sent = kernel(feed, shaped(X * Y * Z, D), (VMEM,) * 6 + (HBM,), late, 16)(
         got, gate_matrix, linear_matrix, gate_other, linear_other, down_matrix, down_other
     )
     got = exchange(sent.reshape(X * Y, Z, D), ("x", "y"))
-    sent = kernel(gather_sum, blocks, rows, 0, 1)(got)
+    sent = kernel(gather_sum, blocks, (VMEM,), rows)(got)
     got = exchange(sent, "z")
-    return kernel(leave, shaped(1, D), (), 0, 3)(got, residual, fold(closing_gain))
+    return kernel(leave, shaped(1, D), (VMEM,) * 3)(got, residual, vectors)
 
 
 def solution(mesh):

time: 151 us -> 125 us (0.83)
  blocking collectives: 33.6 us -> 90.9 us
  waiting for transfers between devices: 45.2 us -> 4.39 us
  starting transfers between devices: 31.1 us -> 12.3 us
  Pallas kernels: 27.6 us -> 9.37 us
  local copies, waits for them, and re-layouts: 9.56 us -> 5.46 us
    all_to_all x2 -> x6, blocking collectives: 33.6 us -> 90.9 us  [exchange(): return lax.all_to_all(blocks, axes, 0, 0, tiled=True)]
    all_to_all x5 -> x1, waiting for transfers between devices: 45.2 us -> 4.38 us  [exchange(): return lax.all_to_all(blocks, axes, 0, 0, tiled=True)]
    all_to_all x5 -> x1, starting transfers between devices: 30.4 us -> 11.6 us  [exchange(): return lax.all_to_all(blocks, axes, 0, 0, tiled=True)]
    pallas_call x7, Pallas kernels: 27.6 us -> 9.37 us  [the longest x1 4.23 us: per_device(): kernel(attend, shaped(PAGES, BEAMS, 5 * HEAD), (SMEM, VMEM, VMEM, HBM, HB...]
    unnamed x20 -> x15, local copies, waits for them, and re-layouts: 3.76 us -> 0.04 us
    reshape x4 -> x0, local copies, waits for them, and re-layouts: 2.49 us -> none  [fold(): return jnp.pad(v.reshape(-1), (0, 8 * FOLD - D)).reshape(8, FOLD)]
    another operation x0 -> x3, local copies, waits for them, and re-layouts: none -> 2.15 us  [per_device(): jnp.stack([stream[0], attention_gain, feedforward_gain, closing_gain])]
  transfers between devices with their start and end apart: 8 -> 4, of which waited for: 5 -> 1; matrix products, arithmetic and copies ran while one was open for 5% -> 5% of each run, Pallas kernels for 6% -> 5%
where the time goes in v3:
time: 125 us
  blocking collectives  90.9 us (73%)
  starting transfers between devices  12.3 us (10%)
  Pallas kernels  9.37 us (7%)
  local copies, waits for them, and re-layouts  5.46 us (4%)
  waiting for transfers between devices  4.39 us (4%)
  other arithmetic  2.05 us (2%)
    all_to_all x6, blocking collectives, exchange(): return lax.all_to_all(blocks, axes, 0, 0, tiled=True)  90.9 us
    all_to_all x1, starting transfers between devices, exchange(): return lax.all_to_all(blocks, axes, 0, 0, tiled=True)  11.6 us
    all_to_all x1, waiting for transfers between devices, exchange(): return lax.all_to_all(blocks, axes, 0, 0, tiled=True)  4.38 us
    pallas_call x1, Pallas kernels, per_device(): kernel(attend, shaped(PAGES, BEAMS, 5 * HEAD), (SMEM, VMEM, VMEM, HBM, HB...  4.23 us
  transfers between devices with their start and end apart: 4, of which 1 were waited for; matrix products, arithmetic and copies ran while one was open for 5% of the time, Pallas kernels for 5%

profile of v3, /device:TPU:2, one launch (start us, length us, event | category | flops | bytes accessed | tf_op | source)
XLA Modules:
  0.0 124.6 jit_solution(13490083112216784217)
XLA Ops:
  0.0 1.4 %broadcast_in_dim.70 = bf16[32,8,512]{2,1,0:T(8,128)(2,1)} broadcast(bf16[8,512]{1,0:T(8,128)(2,1)} %q.1), dimensions={1,2} | broadcast | bytes 270336 | tf_op jit(solution)/shard_map/broadcast_in_dim | solution.py:233
  1.4 11.6 %all-to-all-start = ((bf16[32,8,512]{2,1,0:T(8,128)(2,1)}), bf16[32,8,512]{2,1,0:T(8,128)(2,1)S(1)}, u32[]{:S(2)}, u32[]{:S(2)}) async-start(bf16[32,8,512]{2,1,0:T(8,128)(2,1)} %broadcast_in_dim.70), calls=%async_computation | async-start | bytes 524288 | tf_op jit(solution)/shard_map/all_to_all | solution.py:199
  13.0 0.1 collective-permute-start
  13.1 0.5 collective-permute-start.1
  13.6 0.1 collective-permute-start.2
  13.7 0.7 broadcast_in_dim.62
  14.5 0.1 sub.25
  14.6 0.7 stack.12
  15.3 0.7 stack.13
  16.0 0.7 stack.14
  16.7 0.1 subtract_clamp_fusion
  16.8 0.8 fusion.6
  17.6 0.8 select_reduce_fusion.1
  18.5 0.8 reshape.70
  19.3 0.1 broadcast_in_dim.66
  19.4 0.1 reshape.71
  19.5 0.1 select_reduce_fusion.2.prompt
  19.6 0.2 select_reduce_fusion.valid
  19.9 4.4 %all-to-all-done.q = bf16[32,8,512]{2,1,0:T(8,128)(2,1)S(1)} async-done(((bf16[32,8,512]{2,1,0:T(8,128)(2,1)}), bf16[32,8,512]{2,1,0:T(8,128)(2,1)S(1)}, u32[]{:S(2)}, u32[]{:S(2)}) %all-to-all-start) | async-done | bytes 262176 | tf_op jit(solution)/shard_map/all_to_all | solution.py:199
  24.3 4.2 %attend.1 = bf16[32,8,640]{2,1,0:T(8,128)(2,1)S(1)} custom-call(s32[16]{0:T(128)S(1)} %select_reduce_fusion.2.prompt, s32[8,16]{1,0:T(8,128)S(1)} %select_reduce_fusion.valid, bf16[32,8,512]{2,1,0:T(8,128)(2,1)S(1)} %all-to-all-done.q, bf16[16,256,256]{2,1,0:T(8,128)(2,1)} %k_hbm.1, bf16[16,256,256]{2,1,0:T(8,128)(2,1)} %v_hbm.1), custom_call_target="tpu_custom_call" | custom-call | tf_op jit(solution)/shard_map/attend/pallas_call | solution.py:253
  28.5 18.4 %all_to_all.35.got = bf16[32,8,640]{2,1,0:T(8,128)(2,1)S(1)} all-to-all(bf16[32,8,640]{2,1,0:T(8,128)(2,1)S(1)} %attend.1), channel_id=1, replica_groups=mesh['z'=8,'x'=4,'y'=4,'c'=2] {'z','x'}, dimensions={0} | all-to-all | bytes 655360 | tf_op jit(solution)/shard_map/all_to_all | solution.py:199
  47.0 1.5 %project.1 = bf16[8,8,640]{2,1,0:T(8,128)(2,1)S(1)} custom-call(bf16[32,8,640]{2,1,0:T(8,128)(2,1)S(1)} %all_to_all.35.got, bf16[8,512]{1,0:T(8,128)(2,1)S(1)} %copy-done.4, bf16[8,256]{1,0:T(8,128)(2,1)S(1)} %copy-done.5, bf16[8,256]{1,0:T(8,128)(2,1)S(1)} %copy-done.6, bf16[4608,512]{1,0:T(8,128)(2,1)S(1)} %copy-done), custom_call_target="tpu_custom_call" | custom-call | tf_op jit(solution)/shard_map/project/pallas_call | solution.py:270
  48.5 10.1 %all_to_all.36.got = bf16[8,8,640]{2,1,0:T(8,128)(2,1)S(1)} all-to-all(bf16[8,8,640]{2,1,0:T(8,128)(2,1)S(1)} %project.1), channel_id=1, replica_groups=mesh['z'=8,'x'=4,'y'=4,'c'=2] {'y','c'}, dimensions={0} | all-to-all | bytes 163840 | tf_op jit(solution)/shard_map/all_to_all | solution.py:199
  58.6 0.2 enter.1
  58.8 11.4 %all_to_all.37.got = bf16[8,8,640]{2,1,0:T(8,128)(2,1)S(1)} all-to-all(bf16[8,8,640]{2,1,0:T(8,128)(2,1)S(1)} %get-tuple-element.16), channel_id=1, replica_groups=mesh['z'=8,'x'=4,'y'=4,'c'=2] {'z'}, dimensions={0} | all-to-all | bytes 163840 | tf_op jit(solution)/shard_map/all_to_all | solution.py:199
  70.2 0.2 widen.1
  70.4 20.6 %all_to_all.38 = bf16[16,8,4608]{2,1,0:T(8,128)(2,1)S(1)} all-to-all(bf16[16,8,4608]{2,1,0:T(8,128)(2,1)S(1)} %widen.1), channel_id=1, replica_groups=mesh['z'=8,'x'=4,'y'=4,'c'=2] {'x','y'}, dimensions={0} | all-to-all | bytes 2359296 | tf_op jit(solution)/shard_map/all_to_all | solution.py:199
  91.0 2.3 %feed.1 = bf16[128,4608]{1,0:T(8,128)(2,1)S(1)} custom-call(bf16[128,4608]{1,0:T(8,128)(2,1)S(1)} %bitcast.10, bf16[144,4608]{1,0:T(8,128)(2,1)S(1)} %copy-done.1, bf16[144,4608]{1,0:T(8,128)(2,1)S(1)} %copy-done.2, bf16[144,4608]{1,0:T(8,128)(2,1)S(1)} %collective-permute-done.g1, bf16[144,4608]{1,0:T(8,128)(2,1)S(1)} %collective-permute-done.1.l1, ...), custom_call_target="tpu_custom_call" | custom-call | tf_op jit(solution)/shard_map/feed/pallas_call | solution.py:286
  93.4 19.4 %all_to_all.39.got = bf16[16,8,4608]{2,1,0:T(8,128)(2,1)S(1)} all-to-all(bf16[16,8,4608]{2,1,0:T(8,128)(2,1)S(1)} %bitcast.11), channel_id=1, replica_groups=mesh['z'=8,'x'=4,'y'=4,'c'=2] {'x','y'}, dimensions={0} | all-to-all | bytes 2359296 | tf_op jit(solution)/shard_map/all_to_all | solution.py:199
  112.8 0.2 gather_sum.1
  113.0 10.9 %all_to_all.40.got = bf16[8,8,640]{2,1,0:T(8,128)(2,1)S(1)} all-to-all(bf16[8,8,640]{2,1,0:T(8,128)(2,1)S(1)} %gather_sum.1), channel_id=1, replica_groups=mesh['z'=8,'x'=4,'y'=4,'c'=2] {'z'}, dimensions={0} | all-to-all | bytes 163840 | tf_op jit(solution)/shard_map/all_to_all | solution.py:199
  123.9 0.7 leave.1
  (23 shorter events, 0.1 us)
Async XLA Ops:
  1.4 22.8 %all-to-all-start = ((bf16[32,8,512]{2,1,0:T(8,128)(2,1)}), bf16[32,8,512]{2,1,0:T(8,128)(2,1)S(1)}, u32[]{:S(2)}, u32[]{:S(2)}) async-start(bf16[32,8,512]{2,1,0:T(8,128)(2,1)} %broadcast_in_dim.70), calls=%async_computation | async-start | bytes 524288 | tf_op jit(solution)/shard_map/all_to_all | solution.py:199
  13.0 35.4 %collective-permute-start = (bf16[144,4608]{1,0:T(8,128)(2,1)}, bf16[144,4608]{1,0:T(8,128)(2,1)S(1)}, u32[]{:S(2)}, u32[]{:S(2)}) collective-permute-start(bf16[144,4608]{1,0:T(8,128)(2,1)} %g0.1), channel_id=1, source_target_pairs={{0,1},{1,0},{2,3},{3,2},{4,5},{5,4},{6,7},{7,6},{8,9},{9,8},{10,11... | collective-permute-start | bytes 3981320 | tf_op jit(solution)/shard_map/ppermute | solution.py:229
  13.1 35.3 %collective-permute-start.1 = (bf16[144,4608]{1,0:T(8,128)(2,1)}, bf16[144,4608]{1,0:T(8,128)(2,1)S(1)}, u32[]{:S(2)}, u32[]{:S(2)}) collective-permute-start(bf16[144,4608]{1,0:T(8,128)(2,1)} %l0.1), channel_id=1, source_target_pairs={{0,1},{1,0},{2,3},{3,2},{4,5},{5,4},{6,7},{7,6},{8,9},{9,8},{10,11... | collective-permute-start | bytes 3981320 | tf_op jit(solution)/shard_map/ppermute | solution.py:230
  13.6 34.8 %collective-permute-start.2 = (bf16[144,4608]{1,0:T(8,128)(2,1)}, bf16[144,4608]{1,0:T(8,128)(2,1)}, u32[]{:S(2)}, u32[]{:S(2)}) collective-permute-start(bf16[144,4608]{1,0:T(8,128)(2,1)} %d0.1), channel_id=1, source_target_pairs={{0,1},{1,0},{2,3},{3,2},{4,5},{5,4},{6,7},{7,6},{8,9},{9,8},{10,11... | collective-permute-start | bytes 3981320 | tf_op jit(solution)/shard_map/ppermute | solution.py:231
  24.2 22.7 %copy-start = (bf16[4608,512]{1,0:T(8,128)(2,1)S(1)}, bf16[4608,512]{1,0:T(8,128)(2,1)}, u32[]{:S(2)}) copy-start(bf16[4608,512]{1,0:T(8,128)(2,1)} %wo.1) | copy-start | bytes 14155780
  24.3 22.7 %copy-start.4 = (bf16[8,512]{1,0:T(8,128)(2,1)S(1)}, bf16[8,512]{1,0:T(8,128)(2,1)}, u32[]{:S(2)}) copy-start(bf16[8,512]{1,0:T(8,128)(2,1)} %q.1) | copy-start | bytes 24580
  24.3 22.7 %copy-start.5 = (bf16[8,256]{1,0:T(8,128)(2,1)S(1)}, bf16[8,256]{1,0:T(8,128)(2,1)}, u32[]{:S(2)}) copy-start(bf16[8,256]{1,0:T(8,128)(2,1)} %fresh_k.1) | copy-start | bytes 12292
  24.3 22.7 %copy-start.6 = (bf16[8,256]{1,0:T(8,128)(2,1)S(1)}, bf16[8,256]{1,0:T(8,128)(2,1)}, u32[]{:S(2)}) copy-start(bf16[8,256]{1,0:T(8,128)(2,1)} %fresh_v.1) | copy-start | bytes 12292
  48.5 42.5 %copy-start.3 = (bf16[144,4608]{1,0:T(8,128)(2,1)S(1)}, bf16[144,4608]{1,0:T(8,128)(2,1)}, u32[]{:S(2)}) copy-start(bf16[144,4608]{1,0:T(8,128)(2,1)} %d0.1) | copy-start | bytes 3981316
  70.2 20.8 %copy-start.2 = (bf16[144,4608]{1,0:T(8,128)(2,1)S(1)}, bf16[144,4608]{1,0:T(8,128)(2,1)}, u32[]{:S(2)}) copy-start(bf16[144,4608]{1,0:T(8,128)(2,1)} %l0.1) | copy-start | bytes 3981316
  70.4 20.6 %copy-start.1 = (bf16[144,4608]{1,0:T(8,128)(2,1)S(1)}, bf16[144,4608]{1,0:T(8,128)(2,1)}, u32[]{:S(2)}) copy-start(bf16[144,4608]{1,0:T(8,128)(2,1)} %g0.1) | copy-start | bytes 3981316
